TPU v7x, 32 devices: a whole 2x2x4 slice. The times are simulated.
32 devices in a mesh: rep: 4 (over y, x), shard: 8 (over z, core).
Axes of the slice: x: 2, y: 2, z: 4, core: 2. Of those that a mesh axis runs over, the one named last changes fastest.
Arguments:
- hidden_in: bfloat16 [8, 512, 768], P('shard', 'rep')
- attn_in: bfloat16 [1, 768, 2304], P(None, 'shard')
- attn_out: bfloat16 [1, 768, 768], P(None, 'shard'), may hold values from -4 to 4
- fc_in: bfloat16 [1, 768, 3072], P(None, 'shard'), may hold values from -0.21875 to 0.21875
- fc_out: bfloat16 [1, 3072, 768], P(None, 'shard'), may hold values from -0.109375 to 0.109375
- norm_gains: bfloat16 [1, 2, 768], P(None, None, 'shard'), may hold values from 0.099609375 to 1.8984375
- biases: bfloat16 [1, 6, 768], P(None, None, 'shard'), may hold values from -3 to 3
- fc_in_bias: bfloat16 [1, 3072], P(None, 'shard'), may hold values from -3 to 3
- out_grad: float32 [8, 512, 768], P('shard', 'rep'), may hold values from -6 to 6
Outputs:
- hidden_out: float32 [8, 512, 768], P('shard', 'rep')
- hidden_in_grad: float32 [8, 512, 768], P('shard', 'rep')
- attn_in_grad: float32 [1, 768, 2304], P(None, 'shard')
- attn_out_grad: float32 [1, 768, 768], P(None, 'shard')
- fc_in_grad: float32 [1, 768, 3072], P(None, 'shard')
- fc_out_grad: float32 [1, 3072, 768], P(None, 'shard')
- norm_gains_grad: float32 [1, 2, 768], P(None, None, 'shard')
- biases_grad: float32 [1, 6, 768], P(None, None, 'shard')
- fc_in_bias_grad: float32 [1, 3072], P(None, 'shard')
All inputs are finite; a program needn't handle non-finite values.
Results may differ from a plain program's by a relative error of at most 0.019.
The roundings to bfloat16 on the way count: a program that leaves them out, or rounds other values in their place, can miss the bound.
Values may be sent and summed in bfloat16 or wider, within the bound.
A program may use at most 128 MiB of HBM per device.

v0:
```python
import math

import jax
import jax.numpy as jnp
from jax import lax
from jax.sharding import PartitionSpec as P

H = 12


EPS = 1e-05


def norm_forward(values, gain, shift):
    center = values - jnp.mean(values, axis=-1, keepdims=True)
    inv_root = lax.rsqrt(jnp.mean(center * center, axis=-1, keepdims=True) + EPS)
    normed = center * inv_root
    return (normed * gain + shift, normed, inv_root)


def norm_backward(upstream, gain, normed, inv_root):
    scaled = upstream * gain
    inner = (
        scaled
        - jnp.mean(scaled, axis=-1, keepdims=True)
        - normed * jnp.mean(scaled * normed, axis=-1, keepdims=True)
    )
    return (inv_root * inner, jnp.sum(upstream * normed, axis=0), jnp.sum(upstream, axis=0))


def gelu_slope(pre):
    cdf = 0.5 * (1.0 + lax.erf(pre * (1.0 / math.sqrt(2.0))))
    dens = jnp.exp(-0.5 * pre * pre) * (1.0 / math.sqrt(2.0 * math.pi))
    return cdf + pre * dens


def contract_rows(left, right):
    return lax.dot_general(
        left, right, (((0,), (0,)), ((), ())), preferred_element_type=jnp.float32
    )


def contract_cols(left, right):
    return lax.dot_general(
        left, right, (((1,), (1,)), ((), ())), preferred_element_type=jnp.float32
    )


def split_heads(values):
    return values.reshape(values.shape[0], H, values.shape[1] // H)


def score_block(queries, keys):
    scale = (queries.shape[1] // H) ** (-0.5)
    return (
        jnp.einsum(
            "qhd,khd->hqk",
            split_heads(queries),
            split_heads(keys),
            preferred_element_type=jnp.float32,
        )
        * scale
    )


def attend(queries, keys, values_in):
    scores = score_block(queries, keys)
    top = jnp.max(scores, axis=-1, keepdims=True)
    lse = top[..., 0] + jnp.log(jnp.sum(jnp.exp(scores - top), axis=-1))
    probs = jnp.exp(scores - lse[..., None]).astype(jnp.bfloat16)
    mixed = jnp.einsum(
        "hqk,khd->qhd", probs, split_heads(values_in), preferred_element_type=jnp.float32
    )
    return (mixed.reshape(queries.shape[0], -1).astype(jnp.bfloat16), lse)


def attend_back(queries, keys, values_in, lse, upstream):
    scale = (queries.shape[1] // H) ** (-0.5)
    probs = jnp.exp(score_block(queries, keys) - lse[..., None])
    weights = probs.astype(jnp.bfloat16)
    dprobs = jnp.einsum(
        "qhd,khd->hqk",
        split_heads(upstream),
        split_heads(values_in),
        preferred_element_type=jnp.float32,
    )
    delta = jnp.sum(probs * dprobs, axis=-1, keepdims=True)
    dscores = (probs * (dprobs - delta) * scale).astype(jnp.bfloat16)
    dquery = jnp.einsum(
        "hqk,khd->qhd", dscores, split_heads(keys), preferred_element_type=jnp.float32
    ).reshape(queries.shape[0], -1)
    dkey = jnp.einsum(
        "hqk,qhd->khd", dscores, split_heads(queries), preferred_element_type=jnp.float32
    ).reshape(keys.shape[0], -1)
    dvalue = jnp.einsum(
        "hqk,qhd->khd", weights, split_heads(upstream), preferred_element_type=jnp.float32
    ).reshape(keys.shape[0], -1)
    return (dquery, dkey, dvalue)


def body(hidden_in, attn_in, attn_out, fc_in, fc_out, norm_gains, biases, fc_in_bias, out_grad):
    layers = attn_in.shape[0]
    state = hidden_in[0].astype(jnp.float32)
    layer = 0
    pieces = (
        lax.all_gather(attn_in[layer], "shard", axis=0, tiled=True),
        lax.all_gather(attn_out[layer], "shard", axis=0, tiled=True),
        lax.all_gather(fc_in[layer], "shard", axis=0, tiled=True),
        lax.all_gather(fc_out[layer], "shard", axis=0, tiled=True),
        lax.all_gather(norm_gains[layer], "shard", axis=1, tiled=True),
        lax.all_gather(biases[layer], "shard", axis=1, tiled=True),
        lax.all_gather(fc_in_bias[layer], "shard", axis=0, tiled=True),
    )
    w_qkv = pieces[0]
    w_out = pieces[1]
    w_up = pieces[2]
    w_down = pieces[3]
    gains = pieces[4].astype(jnp.float32)
    shifts = pieces[5].astype(jnp.float32)
    up_bias = pieces[6].astype(jnp.float32)
    width = w_out.shape[0]
    normed_in, normed1, inv1 = norm_forward(state, gains[0], shifts[0])
    a_low = normed_in.astype(jnp.bfloat16)
    qkv = jnp.dot(a_low, w_qkv, preferred_element_type=jnp.float32)
    queries = (qkv[:, :width] + shifts[1]).astype(jnp.bfloat16)
    keys_local = qkv[:, width : 2 * width].astype(jnp.bfloat16)
    values_local = (qkv[:, 2 * width :] + shifts[2]).astype(jnp.bfloat16)
    keys_all = lax.all_gather(keys_local, "rep", axis=0, tiled=True)
    values_all = lax.all_gather(values_local, "rep", axis=0, tiled=True)
    attended, lse = attend(queries, keys_all, values_all)
    mixed = state + jnp.dot(attended, w_out, preferred_element_type=jnp.float32) + shifts[3]
    normed_mid, normed2, inv2 = norm_forward(mixed, gains[1], shifts[4])
    c_low = normed_mid.astype(jnp.bfloat16)
    pre = jnp.dot(c_low, w_up, preferred_element_type=jnp.float32) + up_bias
    act_low = jax.nn.gelu(pre, approximate=False).astype(jnp.bfloat16)
    result = mixed + jnp.dot(act_low, w_down, preferred_element_type=jnp.float32) + shifts[5]
    saved = [
        (
            normed1,
            inv1,
            a_low,
            queries,
            keys_all,
            values_all,
            lse,
            attended,
            normed2,
            inv2,
            c_low,
            pre,
            act_low,
            (w_qkv, w_out, w_up, w_down, gains),
        )
    ]
    upstream = out_grad[0]
    layer_grads = [None] * layers
    for layer in reversed(range(layers)):
        (
            normed1,
            inv1,
            a_low,
            queries,
            keys_all,
            values_all,
            lse,
            attended,
            normed2,
            inv2,
            c_low,
            pre,
            act_low,
            held,
        ) = saved[layer]
        w_qkv, w_out, w_up, w_down, gains = held
        dy_low = upstream.astype(jnp.bfloat16)
        d_down = contract_rows(act_low, dy_low)
        de5 = jnp.sum(upstream, axis=0)
        dact = contract_cols(dy_low, w_down)
        dpre = dact * gelu_slope(pre)
        dpre_low = dpre.astype(jnp.bfloat16)
        d_up = contract_rows(c_low, dpre_low)
        d_up_bias = jnp.sum(dpre, axis=0)
        dmid = contract_cols(dpre_low, w_up)
        dmixed_part, dg2, de4 = norm_backward(dmid, gains[1], normed2, inv2)
        dmixed = upstream + dmixed_part
        dmixed_low = dmixed.astype(jnp.bfloat16)
        d_out = contract_rows(attended, dmixed_low)
        de3 = jnp.sum(dmixed, axis=0)
        dattended = contract_cols(dmixed_low, w_out).astype(jnp.bfloat16)
        dquery, dkey_part, dvalue_part = attend_back(queries, keys_all, values_all, lse, dattended)
        dkey, dvalue = (
            lax.psum_scatter(
                dkey_part.astype(jnp.bfloat16), "rep", scatter_dimension=0, tiled=True
            ).astype(jnp.float32),
            lax.psum_scatter(
                dvalue_part.astype(jnp.bfloat16), "rep", scatter_dimension=0, tiled=True
            ).astype(jnp.float32),
        )
        g_qkv = jnp.concatenate([dquery, dkey, dvalue], axis=1).astype(jnp.bfloat16)
        d_qkv = contract_rows(a_low, g_qkv)
        de1 = jnp.sum(dquery, axis=0)
        de2 = jnp.sum(dvalue, axis=0)
        dnormed = contract_cols(g_qkv, w_qkv)
        dstate_part, dg1, de0 = norm_backward(dnormed, gains[0], normed1, inv1)
        upstream = dmixed + dstate_part
        owned = (
            lax.psum_scatter(
                d_qkv.astype(jnp.bfloat16), "shard", scatter_dimension=0, tiled=True
            ).astype(jnp.float32),
            lax.psum_scatter(
                d_out.astype(jnp.bfloat16), "shard", scatter_dimension=0, tiled=True
            ).astype(jnp.float32),
            lax.psum_scatter(
                d_up.astype(jnp.bfloat16), "shard", scatter_dimension=0, tiled=True
            ).astype(jnp.float32),
            lax.psum_scatter(
                d_down.astype(jnp.bfloat16), "shard", scatter_dimension=0, tiled=True
            ).astype(jnp.float32),
            lax.psum_scatter(
                jnp.stack([dg1, dg2]).astype(jnp.bfloat16), "shard", scatter_dimension=1, tiled=True
            ).astype(jnp.float32),
            lax.psum_scatter(
                jnp.stack([de0, de1, de2, de3, de4, de5]).astype(jnp.bfloat16),
                "shard",
                scatter_dimension=1,
                tiled=True,
            ).astype(jnp.float32),
            lax.psum_scatter(
                d_up_bias.astype(jnp.bfloat16), "shard", scatter_dimension=0, tiled=True
            ).astype(jnp.float32),
        )
        owned = (
            lax.psum(owned[0].astype(jnp.bfloat16), "rep").astype(jnp.float32),
            lax.psum(owned[1].astype(jnp.bfloat16), "rep").astype(jnp.float32),
            lax.psum(owned[2].astype(jnp.bfloat16), "rep").astype(jnp.float32),
            lax.psum(owned[3].astype(jnp.bfloat16), "rep").astype(jnp.float32),
            lax.psum(owned[4].astype(jnp.bfloat16), "rep").astype(jnp.float32),
            lax.psum(owned[5].astype(jnp.bfloat16), "rep").astype(jnp.float32),
            lax.psum(owned[6].astype(jnp.bfloat16), "rep").astype(jnp.float32),
        )
        layer_grads[layer] = owned
    stacked = tuple((jnp.stack([grads[index] for grads in layer_grads]) for index in range(7)))
    return (
        result[None],
        upstream[None],
        stacked[0],
        stacked[1],
        stacked[2],
        stacked[3],
        stacked[4],
        stacked[5],
        stacked[6],
    )


def solution(mesh):
    in_specs = (
        P("shard", "rep", None),
        P(None, "shard", None),
        P(None, "shard", None),
        P(None, "shard", None),
        P(None, "shard", None),
        P(None, None, "shard"),
        P(None, None, "shard"),
        P(None, "shard"),
        P("shard", "rep", None),
    )
    out_specs = (
        P("shard", "rep", None),
        P("shard", "rep", None),
        P(None, "shard", None),
        P(None, "shard", None),
        P(None, "shard", None),
        P(None, "shard", None),
        P(None, None, "shard"),
        P(None, None, "shard"),
        P(None, "shard"),
    )
    return jax.shard_map(body, mesh=mesh, in_specs=in_specs, out_specs=out_specs, check_vma=False)
```

profile of v0, /device:TPU:0, one launch (start us, length us, event | category | flops | bytes accessed | tf_op | source)
XLA Modules:
  0.0 602.9 jit_solution(12913326012908894755)
XLA Ops:
  10.2 16.9 %all-gather.1 = bf16[1,6,768]{1,0,2:T(2,128)(2,1)S(1)} all-gather(bf16[1,6,96]{1,0,2:T(2,128)(2,1)S(1)} %copy.38), channel_id=3, replica_groups=mesh['rep'=4,'shard'=8] {'shard'}, dimensions={2}, use_global_device_ids=true | all-gather | bytes 10368 | tf_op jit(solution)/shard_map/all_gather | solution.py:111
  27.7 16.6 %all-gather = bf16[1,2,768]{1,0,2:T(2,128)(2,1)S(1)} all-gather(bf16[1,2,96]{1,0,2:T(2,128)(2,1)S(1)} %copy.37), channel_id=2, replica_groups=mesh['rep'=4,'shard'=8] {'shard'}, dimensions={2}, use_global_device_ids=true | all-gather | bytes 3456 | tf_op jit(solution)/shard_map/all_gather | solution.py:110
  44.7 13.8 %all-gather.5 = bf16[1,3072]{1,0:T(2,128)(2,1)S(1)} all-gather(bf16[1,384]{1,0:T(2,128)(2,1)S(1)} %copy-done.35), channel_id=7, replica_groups=mesh['rep'=4,'shard'=8] {'shard'}, dimensions={1}, use_global_device_ids=true | all-gather | bytes 6912 | tf_op jit(solution)/shard_map/all_gather | solution.py:112
  59.4 4.6 slice_reduce_fusion.2
  64.0 13.3 %slice_reduce_fusion = (f32[768]{0:T(1024)}, f32[768]{0:T(1024)S(1)}, f32[768]{0:T(1024)}, f32[768]{0:T(1024)S(1)}, f32[768]{0:T(1024)S(1)}, /*index=5*/f32[768]{0:T(1024)S(1)}) fusion(f32[1,6,768]{1,0,2:T(1,128)S(1)} %convert_element_type.152), kind=kLoop, calls=%fused_computation.88 | loop fusion | bytes 36864 | tf_op jit(solution)/shard_map/slice | solution.py:136
  77.3 2.7 fusion.17
  80.3 12.4 %all_gather.31 = bf16[512,768]{1,0:T(8,128)(2,1)S(1)} all-gather(bf16[128,768]{1,0:T(8,128)(2,1)S(1)} %slice.81), channel_id=1, replica_groups=mesh['rep'=4,'shard'=8] {'rep'}, dimensions={0}, use_global_device_ids=true | all-gather | bytes 983040 | tf_op jit(solution)/shard_map/all_gather | solution.py:128
  93.9 11.7 %all_gather.30 = bf16[512,768]{1,0:T(8,128)(2,1)S(1)} all-gather(bf16[128,768]{1,0:T(8,128)(2,1)S(1)} %get-tuple-element.53), channel_id=1, replica_groups=mesh['rep'=4,'shard'=8] {'rep'}, dimensions={0}, use_global_device_ids=true | all-gather | bytes 983040 | tf_op jit(solution)/shard_map/all_gather | solution.py:129
  114.4 19.3 %all-gather.16.cloned.1.call-done = bf16[1,768,3072]{2,1,0:T(8,128)(2,1)} async-done(((bf16[1,96,3072]{2,1,0:T(8,128)(2,1)}), bf16[1,768,3072]{2,1,0:T(8,128)(2,1)}) %all-gather.16.cloned.1.call-update) | async-done | bytes 4718608 | tf_op jit(solution)/shard_map/all_gather | solution.py:108
  133.7 7.9 %fusion.31 = (bf16[128,3072]{1,0:T(8,128)(2,1)}, f32[128,3072]{1,0:T(8,128)}) fusion(f32[3072]{0:T(1024)} %bitcast.174, bf16[1,768,3072]{2,1,0:T(8,128)(2,1)} %all-gather.16.cloned.1.call-done, f32[128,768]{1,0:T(8,128)S(1)} %get-tuple-element.59, f32[768]{0:T(1024)S(1)} %get-tuple-element.36, f32[768]{0:T(1024)S(1)} %get-tuple-element.41, ...), kind=kOutput, calls=%fused_computation.31 | convolution fusion | flops 630423552 | bytes 7490560 | tf_op jit(solution)/shard_map/dot_general | solution.py:134
  141.6 43.6 %all-gather.18.cloned.1.call-done = bf16[1,3072,768]{2,1,0:T(8,128)(2,1)} async-done(((bf16[1,384,768]{2,1,0:T(8,128)(2,1)}), bf16[1,3072,768]{2,1,0:T(8,128)(2,1)}) %all-gather.18.cloned.1.call-update) | async-done | bytes 4718608 | tf_op jit(solution)/shard_map/all_gather | solution.py:109
  185.2 5.4 fusion.116
  197.4 3.5 fusion.122
  201.0 12.9 %fusion.51 = bf16[12,64,512]{2,1,0:T(8,128)(2,1)} fusion(bf16[128,12,64]{0,2,1:T(8,128)(2,1)} %bitcast.162, f32[12,128,512]{2,1,0:T(8,128)} %fusion.122, f32[12,128,512]{2,1,0:T(8,128)S(1)} %get-tuple-element.57, f32[12,128]{1,0:T(8,128)} %copy-done.18), kind=kOutput, calls=%fused_computation.56 | convolution fusion | flops 108136448 | bytes 7280640 | tf_op jit(solution)/shard_map/hqk,qhd->khd/dot_general | solution.py:92
  216.3 2.6 convolution_convert_fusion.4
  224.0 13.2 %fusion.112 = (bf16[12,64]{1,0:T(8,128)(2,1)}, bf16[128,12,64]{0,2,1:T(8,128)(2,1)}) fusion(bf16[512,12,64]{0,2,1:T(8,128)(2,1)} %bitcast.155, f32[12,128,512]{2,1,0:T(8,128)} %fusion.122, f32[12,128,512]{2,1,0:T(8,128)S(1)} %get-tuple-element.57, f32[12,128]{1,0:T(8,128)} %copy-done.18), kind=kOutput, calls=%fused_computation.133 | convolution fusion | flops 107939072 | bytes 7282176 | tf_op jit(solution)/shard_map/hqk,khd->qhd/dot_general | solution.py:89
  237.2 4.3 reduce-scatter.25.cloned.1.call-done
  242.5 27.8 %reduce-scatter.27.cloned.1.call-done = bf16[128,768]{1,0:T(8,128)(2,1)} async-done(((bf16[512,768]{1,0:T(8,128)(2,1)}), bf16[128,768]{1,0:T(8,128)(2,1)}) %reduce-scatter.27.cloned.1.call-update) | async-done | bytes 196624
  271.4 4.0 convolution_convert_fusion.2
  276.6 3.7 convolution_convert_fusion.1
  281.5 3.7 fusion.118
  286.2 3.5 fusion.87
  291.9 14.3 %reduce-scatter.19.cloned.1.call-done = bf16[96,768]{1,0:T(8,128)(2,1)} async-done(((bf16[768,768]{1,0:T(8,128)(2,1)}), bf16[96,768]{1,0:T(8,128)(2,1)}) %reduce-scatter.19.cloned.1.call-update) | async-done | bytes 147472 | tf_op jit(solution)/shard_map/reduce_scatter | solution.py:210
  306.2 44.3 %reduce-scatter.17.cloned.1.call-done = bf16[96,2304]{1,0:T(8,128)(2,1)} async-done(((bf16[768,2304]{1,0:T(8,128)(2,1)}), bf16[96,2304]{1,0:T(8,128)(2,1)}) %reduce-scatter.17.cloned.1.call-update) | async-done | bytes 442384 | tf_op jit(solution)/shard_map/reduce_scatter | solution.py:207
  350.4 55.8 %reduce-scatter.21.cloned.1.call-done = bf16[96,3072]{1,0:T(8,128)(2,1)} async-done(((bf16[768,3072]{1,0:T(8,128)(2,1)}), bf16[96,3072]{1,0:T(8,128)(2,1)}) %reduce-scatter.21.cloned.1.call-update) | async-done | bytes 589840 | tf_op jit(solution)/shard_map/reduce_scatter | solution.py:213
  406.2 55.5 %reduce-scatter.23.cloned.1.call-done = bf16[384,768]{1,0:T(8,128)(2,1)} async-done(((bf16[3072,768]{1,0:T(8,128)(2,1)}), bf16[384,768]{1,0:T(8,128)(2,1)}) %reduce-scatter.23.cloned.1.call-update) | async-done | bytes 589840 | tf_op jit(solution)/shard_map/reduce_scatter | solution.py:216
  463.0 13.9 %all-reduce = bf16[3072]{0:T(1024)(128)(2,1)S(1)} all-reduce(bf16[3072]{0:T(1024)(128)(2,1)S(1)} %copy-done.32), channel_id=17, replica_groups=mesh['rep'=4,'shard'=8] {'shard'}, use_global_device_ids=true, to_apply=%region_34.0.clone | all-reduce | flops 3072 | bytes 12288
  477.1 3.9 fusion.64
  482.0 11.8 %reduce-scatter.29.cloned.1.call-done = bf16[96,2]{1,0:T(8,128)(2,1)} async-done(((bf16[768,2]{1,0:T(8,128)(2,1)}), bf16[96,2]{1,0:T(8,128)(2,1)}) %reduce-scatter.29.cloned.1.call-update) | async-done | bytes 400
  494.5 30.8 %reduce-scatter.31.cloned.1.call-done = bf16[96,6]{1,0:T(8,128)(2,1)} async-done(((bf16[768,6]{1,0:T(8,128)(2,1)}), bf16[96,6]{1,0:T(8,128)(2,1)}) %reduce-scatter.31.cloned.1.call-update) | async-done | bytes 1168
  526.2 9.9 %all-reduce.1 = (bf16[1,2,96]{2,1,0:T(2,128)(2,1)S(1)}, bf16[1,6,96]{2,1,0:T(8,128)(2,1)S(1)}, bf16[1,384]{1,0:T(2,128)(2,1)S(1)}) all-reduce(bf16[1,2,96]{2,1,0:T(2,128)(2,1)S(1)} %bitcast.176, bf16[1,6,96]{2,1,0:T(8,128)(2,1)S(1)} %bitcast.175, bf16[1,384]{1,0:T(2,128)(2,1)S(1)} %stack.104), channel_id=1, replica_groups=mesh['rep'=4,'shard'=8] {'rep'}, use_global_device_ids=true, to_apply=%region_24.0 | all-reduce | flops 1152 | bytes 4608 | tf_op jit(solution)/shard_map/psum | solution.py:237
  537.8 53.3 %all-reduce.5.cloned.1.call-done = (bf16[1,96,2304]{2,1,0:T(8,128)(2,1)}, bf16[1,96,768]{2,1,0:T(8,128)(2,1)}, bf16[1,96,3072]{2,1,0:T(8,128)(2,1)}, bf16[1,384,768]{2,1,0:T(8,128)(2,1)}) async-done(((bf16[1,96,2304]{2,1,0:T(8,128)(2,1)}, bf16[1,96,768]{2,1,0:T(8,128)(2,1)}, bf16[1,96,3072]{2,1,0:T(8,128)(2,1)}, bf16[1,384,768]{2,1,0:T(8,128)(2,1)}), (bf16[1,96,2304]{2,1,0:T(8,128)(2,1)}, ...) | async-done | bytes 1769488 | tf_op jit(solution)/shard_map/psum | solution.py:233
  (165 shorter events, 46.8 us)
Async XLA Ops:
  7.2 2.9 copy-start.34
  7.2 20.4 %copy-start.36 = (bf16[1,2,96]{2,1,0:T(2,128)(2,1)S(1)}, bf16[1,2,96]{2,1,0:T(2,128)(2,1)}, u32[]{:S(2)}) copy-start(bf16[1,2,96]{2,1,0:T(2,128)(2,1)} %param.14) | copy-start | bytes 1156
  7.2 70.1 %all-gather.12.cloned.1.call-start = ((), (), s32[]{:S(2)}) async-start(), calls=%async_computation.12 | async-start | bytes 3981312 | tf_op jit(solution)/shard_map/all_gather | solution.py:106
  7.9 103.4 %all-gather.14.cloned.1.call-start = ((), (), s32[]{:S(2)}) async-start(), calls=%async_computation.13 | async-start | bytes 1327104 | tf_op jit(solution)/shard_map/all_gather | solution.py:107
  8.7 125.0 %all-gather.16.cloned.1.call-start = ((), (), s32[]{:S(2)}) async-start(), calls=%async_computation.14 | async-start | bytes 5308416 | tf_op jit(solution)/shard_map/all_gather | solution.py:108
  9.4 35.2 %copy-start.35 = (bf16[1,384]{1,0:T(2,128)(2,1)S(1)}, bf16[1,384]{1,0:T(2,128)(2,1)}, u32[]{:S(2)}) copy-start(bf16[1,384]{1,0:T(2,128)(2,1)} %param.16) | copy-start | bytes 2308
  9.4 49.6 %copy-start = (bf16[1,128,768]{2,1,0:T(8,128)(2,1)S(1)}, bf16[1,128,768]{2,1,0:T(8,128)(2,1)}, u32[]{:S(2)}) copy-start(bf16[1,128,768]{2,1,0:T(8,128)(2,1)} %param.9) | copy-start | bytes 589828
  9.4 175.7 %all-gather.18.cloned.1.call-start = ((), (), s32[]{:S(2)}) async-start(), calls=%async_computation.15 | async-start | bytes 5308416 | tf_op jit(solution)/shard_map/all_gather | solution.py:109
  10.0 231.4 %reduce-scatter.25.cloned.1.call-start = ((), (), s32[]{:S(2)}) async-start(), calls=%async_computation.16 | async-start | bytes 983040
  59.2 18.1 %copy-start.23 = (f32[128]{0:T(128)}, f32[128]{0:T(128)S(1)}, u32[]{:S(2)}) copy-start(f32[128]{0:T(128)S(1)} %broadcast_multiply_fusion.5) | copy-start | bytes 1540
  64.0 16.1 %copy-start.30 = (f32[128]{0:T(128)}, f32[128]{0:T(128)S(1)}, u32[]{:S(2)}) copy-start(f32[128]{0:T(128)S(1)} %add_rsqrt_fusion.1) | copy-start | bytes 1540
  80.3 26.5 %copy-start.12 = (bf16[128,768]{0,1:T(8,128)(2,1)}, bf16[128,768]{0,1:T(8,128)(2,1)S(1)}, u32[]{:S(2)}) copy-start(bf16[128,768]{0,1:T(8,128)(2,1)S(1)} %copy.40) | copy-start | bytes 589828
  185.2 5.4 copy-start.6
  185.2 5.4 copy-start.21
  185.2 5.4 copy-start.25
  216.2 54.1 %reduce-scatter.27.cloned.1.call-start = ((), (), s32[]{:S(2)}) async-start(), calls=%async_computation.17 | async-start | bytes 983040
  221.3 84.9 %reduce-scatter.19.cloned.1.call-start = ((), (), s32[]{:S(2)}) async-start(), calls=%async_computation.9 | async-start | bytes 1327104 | tf_op jit(solution)/shard_map/reduce_scatter | solution.py:210
  223.9 126.5 %reduce-scatter.17.cloned.1.call-start = ((), (), s32[]{:S(2)}) async-start(), calls=%async_computation.8 | async-start | bytes 3981312 | tf_op jit(solution)/shard_map/reduce_scatter | solution.py:207
  275.5 130.7 %reduce-scatter.21.cloned.1.call-start = ((), (), s32[]{:S(2)}) async-start(), calls=%async_computation.10 | async-start | bytes 5308416 | tf_op jit(solution)/shard_map/reduce_scatter | solution.py:213
  280.3 181.5 %reduce-scatter.23.cloned.1.call-start = ((), (), s32[]{:S(2)}) async-start(), calls=%async_computation.11 | async-start | bytes 5308416 | tf_op jit(solution)/shard_map/reduce_scatter | solution.py:216
  285.2 208.5 %reduce-scatter.29.cloned.1.call-start = ((), (), s32[]{:S(2)}) async-start(), calls=%async_computation.18 | async-start | bytes 221184
  286.2 4.5 copy-start.33
  286.2 4.6 copy-start.28
  286.2 4.6 copy-start.27
  286.2 4.7 copy-start.13
  290.6 171.2 %copy-start.37 = (u32[32]{0:T(128)S(1)}, u32[32]{0:T(128)}, u32[]{:S(2)}) copy-start(u32[32]{0:T(128)} %constant.86) | copy-start | bytes 388
  290.6 172.4 %copy-start.32 = (bf16[3072]{0:T(1024)(128)(2,1)S(1)}, bf16[3072]{0:T(1024)(128)(2,1)}, u32[]{:S(2)}) copy-start(bf16[3072]{0:T(1024)(128)(2,1)} %get-tuple-element.65) | copy-start | bytes 18436
  290.6 186.5 %copy-start.19 = (f32[768]{0:T(1024)S(1)}, f32[768]{0:T(1024)}, u32[]{:S(2)}) copy-start(f32[768]{0:T(1024)} %get-tuple-element.35) | copy-start | bytes 9220
  290.6 234.7 %reduce-scatter.31.cloned.1.call-start = ((), (), s32[]{:S(2)}) async-start(), calls=%async_computation.19 | async-start | bytes 221184
  291.9 299.2 %all-reduce.5.cloned.1.call-start = ((), (), s32[]{:S(2)}) async-start(), calls=%async_computation.20 | async-start | bytes 3538944 | tf_op jit(solution)/shard_map/psum | solution.py:233
  477.1 3.9 copy-start.4
  591.1 3.4 copy-start.15
  (19 other events, 25.2 us)
Sparse Core Ops, SparseCore 0:
  9.6 48.0 all-gather.11
  59.3 21.7 all-gather.13
  82.8 50.8 all-gather.15
  135.2 49.9 all-gather.17
  216.3 25.0 reduce-scatter.24
  244.2 26.1 reduce-scatter.26
  273.2 32.9 reduce-scatter.18
  308.5 41.8 reduce-scatter.16
  352.8 53.4 reduce-scatter.20
  408.4 53.3 reduce-scatter.22
  464.6 29.1 reduce-scatter.28
  496.4 28.9 reduce-scatter.30
  528.8 62.2 all-reduce.4
where the time goes:
time: 606 us; the launch traced here: 603 us
  waiting for transfers between devices  363 us (60%)
  blocking collectives  95.3 us (16%)
  matrix products  78.3 us (13%)
  local copies, waits for them, and re-layouts  38.6 us (6%)
  between operations  15.2 us (3%)
  other arithmetic  11.4 us (2%)
    unnamed x17, waiting for transfers between devices  77.4 us
    reduce_scatter x1, waiting for transfers between devices, body(): lax.psum_scatter(d_up.astype(jnp.bfloat16), 'shard', scatter_dimension=0,...  55.8 us
    reduce_scatter x1, waiting for transfers between devices, body(): lax.psum_scatter(d_down.astype(jnp.bfloat16), 'shard', scatter_dimension=...  55.5 us
    psum x1, waiting for transfers between devices, body(): lax.psum(owned[0].astype(jnp.bfloat16), 'rep').astype(jnp.float32)  53.3 us
    reduce_scatter x1, waiting for transfers between devices, body(): lax.psum_scatter(d_qkv.astype(jnp.bfloat16), 'shard', scatter_dimension=0...  44.3 us
    all_gather x1, waiting for transfers between devices, body(): lax.all_gather(fc_out[layer], 'shard', axis=0, tiled=True)  43.6 us
    all_gather x1, waiting for transfers between devices, body(): lax.all_gather(fc_in[layer], 'shard', axis=0, tiled=True)  19.3 us
    all_gather x1, blocking collectives, body(): lax.all_gather(biases[layer], 'shard', axis=1, tiled=True)  16.9 us
  transfers between devices with their start and end apart: 13, of which 11 were waited for; matrix products, arithmetic and copies ran while one was open for 15% of the time, Pallas kernels for 0%

commit v1 on v0

--- a/solution.py
+++ b/solution.py
@@ -1,11 +1,17 @@
+import functools
 import math
 
 import jax
 import jax.numpy as jnp
 from jax import lax
+from jax.experimental import pallas as pl
+from jax.experimental.pallas import tpu as pltpu
 from jax.sharding import PartitionSpec as P
 
 H = 12
+
+BF16 = jnp.bfloat16
+F32 = jnp.float32
 
 
 EPS = 1e-05
@@ -253,7 +259,282 @@
     )
 
 
+def exchange_body(plan, sizes, *refs):
+    count = len(plan)
+    ins, outs = refs[:count], refs[count : 2 * count]
+    send_sem, recv_sem = refs[2 * count :]
+    me = {axis: lax.axis_index(axis) for axis in sizes}
+    barrier = pltpu.get_barrier_semaphore()
+    greeted = 0
+    for axis in sorted({axis for axis, _ in plan}):
+        for step in range(1, sizes[axis]):
+            peer = lax.rem(me[axis] + step, sizes[axis])
+            pl.semaphore_signal(
+                barrier, inc=1, device_id={axis: peer}, device_id_type=pl.DeviceIdType.MESH
+            )
+            greeted += 1
+    pl.semaphore_wait(barrier, greeted)
+
+    def copy(item, slot, source, target, axis, peer):
+        return pltpu.make_async_remote_copy(
+            src_ref=source,
+            dst_ref=target,
+            send_sem=send_sem.at[item, slot],
+            recv_sem=recv_sem.at[item, slot],
+            device_id={axis: peer},
+            device_id_type=pl.DeviceIdType.MESH,
+        )
+
+    copies = []
+    relays = []
+    for item, (axis, kind) in enumerate(plan):
+        size = sizes[axis]
+        if kind == "relay":
+            half = size // 2
+            core = lax.rem(me[axis], 2)
+            place = me[axis] // 2
+            sibling = me[axis] + 1 - 2 * core
+            for step in range(1, half):
+                peer = lax.rem(place + step, half) * 2 + core
+                first = copy(item, step, ins[item], outs[item].at[me[axis]], axis, peer)
+                first.start()
+                origin = lax.rem(place + half - step, half) * 2 + core
+                relays.append((item, step, first, axis, sibling, origin))
+            own = copy(item, 0, ins[item], outs[item].at[me[axis]], axis, sibling)
+            own.start()
+            copies.append(own)
+        else:
+            for step in range(1, size):
+                peer = lax.rem(me[axis] + step, size)
+                source = ins[item] if kind == "gather" else ins[item].at[peer]
+                one = copy(item, step, source, outs[item].at[me[axis]], axis, peer)
+                one.start()
+                copies.append(one)
+    for item, (axis, kind) in enumerate(plan):
+        if kind == "swap":
+            outs[item][me[axis]] = ins[item][me[axis]]
+        else:
+            outs[item][me[axis]] = ins[item][...]
+    for item, step, first, axis, sibling, origin in relays:
+        first.wait_recv()
+        block = outs[item].at[origin]
+        second = copy(item, sizes[axis] // 2 + step, block, block, axis, sibling)
+        second.start()
+        copies.append(second)
+    for one in copies:
+        one.wait()
+    for _, _, first, _, _, _ in relays:
+        first.wait_send()
+
+
+def exchange(sizes, number, *items):
+    plan = tuple((axis, kind) for _, axis, kind in items)
+    arrays = [array for array, _, _ in items]
+    shapes = []
+    for array, axis, kind in items:
+        shape = array.shape if kind == "swap" else (sizes[axis],) + array.shape
+        shapes.append(jax.ShapeDtypeStruct(shape, array.dtype))
+    slots = max(sizes[axis] for axis, _ in plan)
+    vmem = pl.BlockSpec(memory_space=pltpu.VMEM)
+    return pl.pallas_call(
+        functools.partial(exchange_body, plan, sizes),
+        out_shape=shapes,
+        in_specs=[vmem] * len(arrays),
+        out_specs=[vmem] * len(arrays),
+        scratch_shapes=[
+            pltpu.SemaphoreType.DMA((len(arrays), slots)),
+            pltpu.SemaphoreType.DMA((len(arrays), slots)),
+        ],
+        compiler_params=pltpu.CompilerParams(collective_id=number, has_side_effects=True),
+    )(*arrays)
+
+
+def flat(blocks):
+    return blocks.reshape((blocks.shape[0] * blocks.shape[1],) + blocks.shape[2:])
+
+
+def split_body(
+    sizes, hidden_in, attn_in, attn_out, fc_in, fc_out, norm_gains, biases, fc_in_bias, out_grad
+):
+    reps, shards = sizes["rep"], sizes["shard"]
+    rank = lax.axis_index("rep")
+    rows = hidden_in.shape[1]
+    width = attn_out.shape[2]
+    part = attn_out.shape[1]
+    cols = width // reps
+    units = fc_in.shape[2]
+    share = units // reps
+    piece = fc_out.shape[1] // reps
+    heads = H // reps
+    scale = (width // H) ** (-0.5)
+
+    def mine(array, axis):
+        return lax.dynamic_index_in_dim(array, rank, axis, keepdims=False)
+
+    state = hidden_in[0].astype(F32)
+    upstream = out_grad[0]
+    w_in_part = mine(attn_in[0].reshape(part, 3, reps, cols), 2).reshape(part, 3 * cols)
+    w_up_part = mine(fc_in[0].reshape(part, shards, reps, piece), 2).reshape(part, share)
+    w_down_part = mine(fc_out[0].reshape(reps, piece, width), 0)
+    small = jnp.concatenate(
+        [norm_gains[0].reshape(1, -1), biases[0].reshape(1, -1), fc_in_bias[0].reshape(1, -1)], axis=1
+    )
+    w_out = lax.all_gather(attn_out[0], "shard", axis=0, tiled=True)
+    w_up = lax.all_gather(w_up_part, "shard", axis=0, tiled=True)
+    w_down = lax.all_gather(w_down_part, "shard", axis=0, tiled=True)
+    w_in, small, x_all, dy_low = exchange(
+        sizes,
+        0,
+        (w_in_part, "shard", "relay"),
+        (small, "shard", "gather"),
+        (hidden_in[0], "rep", "gather"),
+        (upstream.astype(BF16), "rep", "gather"),
+    )
+    w_in, x_all, dy_low = flat(w_in), flat(x_all), flat(dy_low)
+    small = small[:, 0, :].astype(F32)
+    gains = small[:, : 2 * part].reshape(shards, 2, part).swapaxes(0, 1).reshape(2, width)
+    shifts = small[:, 2 * part : 8 * part].reshape(shards, 6, part).swapaxes(0, 1).reshape(6, width)
+    up_bias = mine(small[:, 8 * part :].reshape(shards, reps, piece), 1).reshape(share)
+
+    normed_all, normed1_all, inv1_all = norm_forward(x_all.astype(F32), gains[0], shifts[0])
+    a_low = normed_all.astype(BF16)
+    _, normed1, inv1 = norm_forward(state, gains[0], shifts[0])
+    qkv = jnp.dot(a_low, w_in, preferred_element_type=F32)
+
+    def heads_of(values):
+        return values.reshape(values.shape[0], heads, cols // heads)
+
+    queries = heads_of((qkv[:, :cols] + mine(shifts[1].reshape(reps, cols), 0)).astype(BF16))
+    keys = heads_of(qkv[:, cols : 2 * cols].astype(BF16))
+    values_in = heads_of(
+        (qkv[:, 2 * cols :] + mine(shifts[2].reshape(reps, cols), 0)).astype(BF16)
+    )
+    scores = jnp.einsum("qhd,khd->hqk", queries, keys, preferred_element_type=F32) * scale
+    top = jnp.max(scores, axis=-1, keepdims=True)
+    lse = top + jnp.log(jnp.sum(jnp.exp(scores - top), axis=-1, keepdims=True))
+    probs = jnp.exp(scores - lse)
+    weights = probs.astype(BF16)
+    attended = jnp.einsum("hqk,khd->qhd", weights, values_in, preferred_element_type=F32)
+    attended = attended.reshape(reps * rows, cols).astype(BF16)
+    (o_all,) = exchange(sizes, 1, (attended, "rep", "gather"))
+    o_rows = lax.dynamic_slice_in_dim(o_all, rank * rows, rows, 1)
+    o_rows = o_rows.swapaxes(0, 1).reshape(rows, width)
+    mixed = state + jnp.dot(o_rows, w_out, preferred_element_type=F32) + shifts[3]
+    normed_mid, normed2, inv2 = norm_forward(mixed, gains[1], shifts[4])
+    (c_low,) = exchange(sizes, 2, (normed_mid.astype(BF16), "rep", "gather"))
+    c_low = flat(c_low)
+    pre = jnp.dot(c_low, w_up, preferred_element_type=F32) + up_bias
+    act_low = jax.nn.gelu(pre, approximate=False).astype(BF16)
+    y_part = jnp.dot(act_low, w_down, preferred_element_type=F32).astype(BF16)
+
+    d_down = contract_rows(act_low, dy_low)
+    dpre = contract_cols(dy_low, w_down) * gelu_slope(pre)
+    dpre_low = dpre.astype(BF16)
+    d_up_bias = jnp.sum(dpre, axis=0)
+    dmid_part = contract_cols(dpre_low, w_up).astype(BF16)
+    d_up = contract_rows(c_low, dpre_low)
+    ff_grads = lax.psum_scatter(
+        jnp.concatenate([d_up.astype(BF16), d_down.astype(BF16)], axis=1),
+        "shard",
+        scatter_dimension=0,
+        tiled=True,
+    )
+    dmid_parts, y_parts = exchange(
+        sizes,
+        3,
+        (dmid_part.reshape(reps, rows, width), "rep", "swap"),
+        (y_part.reshape(reps, rows, width), "rep", "swap"),
+    )
+    result = mixed + jnp.sum(y_parts.astype(F32), axis=0) + shifts[5]
+    dmid = jnp.sum(dmid_parts.astype(F32), axis=0)
+    de5 = jnp.sum(upstream, axis=0)
+    dmixed_part, dg2, de4 = norm_backward(dmid, gains[1], normed2, inv2)
+    dmixed = upstream + dmixed_part
+    de3 = jnp.sum(dmixed, axis=0)
+    (dmixed_low,) = exchange(sizes, 4, (dmixed.astype(BF16), "rep", "gather"))
+    dmixed_low = flat(dmixed_low)
+    w_out_rows = mine(w_out.reshape(reps, cols, width), 0)
+    dattended = heads_of(contract_cols(dmixed_low, w_out_rows).astype(BF16))
+    dmixed_cols = mine(dmixed_low.reshape(reps * rows, reps, cols), 1)
+    d_out = jnp.einsum("rtc,td->rcd", o_all, dmixed_cols, preferred_element_type=F32)
+    d_out = d_out.reshape(width, cols)
+
+    dprobs = jnp.einsum("qhd,khd->hqk", dattended, values_in, preferred_element_type=F32)
+    delta = jnp.sum(probs * dprobs, axis=-1, keepdims=True)
+    dscores = (probs * (dprobs - delta) * scale).astype(BF16)
+    dquery = jnp.einsum("hqk,khd->qhd", dscores, keys, preferred_element_type=F32)
+    dkey = jnp.einsum("hqk,qhd->khd", dscores, queries, preferred_element_type=F32)
+    dvalue = jnp.einsum("hqk,qhd->khd", weights, dattended, preferred_element_type=F32)
+    g_qkv = jnp.stack([dquery, dkey, dvalue], axis=1).reshape(reps * rows, 3 * cols)
+    de1 = jnp.sum(dquery, axis=0).reshape(cols)
+    de2 = jnp.sum(dvalue, axis=0).reshape(cols)
+    g_qkv = g_qkv.astype(BF16)
+    dnormed_part = contract_cols(g_qkv, w_in).astype(BF16)
+    d_qkv = contract_rows(a_low, g_qkv)
+    attn_grads = jnp.concatenate([d_qkv.astype(BF16), d_out.astype(BF16)], axis=1)
+    dnormed_parts, attn_parts = exchange(
+        sizes,
+        5,
+        (dnormed_part.reshape(reps, rows, width), "rep", "swap"),
+        (attn_grads.reshape(shards, part, width), "shard", "swap"),
+    )
+    attn_sum = jnp.sum(attn_parts.astype(F32), axis=0).astype(BF16)
+    dnormed = jnp.sum(dnormed_parts.astype(F32), axis=0)
+    dstate_part, dg1, de0 = norm_backward(dnormed, gains[0], normed1, inv1)
+    dstate = dmixed + dstate_part
+
+    def placed(values):
+        spread = jnp.zeros((reps, values.shape[0]), F32)
+        return lax.dynamic_update_slice_in_dim(spread, values[None], rank, 0).reshape(-1)
+
+    full = jnp.stack([dg1, dg2, de0, placed(de1), placed(de2), de3, de4, de5])
+    full = full.reshape(8, shards, part).swapaxes(0, 1).reshape(shards, 8 * part)
+    bias_parts = d_up_bias.reshape(shards, 1, piece)
+    bias_parts = lax.dynamic_update_slice_in_dim(
+        jnp.zeros((shards, reps, piece), F32), bias_parts, rank, 1
+    ).reshape(shards, reps * piece)
+    vectors = jnp.concatenate([full, bias_parts], axis=1)[:, None, :]
+    ff_all, attn_all, vectors = exchange(
+        sizes,
+        6,
+        (ff_grads, "rep", "gather"),
+        (attn_sum, "rep", "gather"),
+        (vectors, "shard", "swap"),
+    )
+    (vectors,) = exchange(sizes, 7, (jnp.sum(vectors, axis=0), "rep", "gather"))
+    vectors = jnp.sum(vectors, axis=0).reshape(-1)
+    attn_all, ff_all = attn_all.astype(F32), ff_all.astype(F32)
+    g_attn_in = attn_all[:, :, : 3 * cols].reshape(reps, part, 3, cols)
+    g_attn_in = g_attn_in.transpose(1, 2, 0, 3).reshape(part, 3 * width)
+    g_attn_out = attn_all[:, :, 3 * cols :].swapaxes(0, 1).reshape(part, width)
+    g_fc_in = ff_all[:, :, :share].reshape(reps, part, shards, piece)
+    g_fc_in = g_fc_in.transpose(1, 2, 0, 3).reshape(part, units)
+    g_fc_out = ff_all[:, :, share:].reshape(reps * piece, width)
+    return (
+        result[None],
+        dstate[None],
+        g_attn_in[None],
+        g_attn_out[None],
+        g_fc_in[None],
+        g_fc_out[None],
+        vectors[: 2 * part].reshape(1, 2, part),
+        vectors[2 * part : 8 * part].reshape(1, 6, part),
+        vectors[8 * part :][None],
+    )
+
+
+def run(sizes, *args):
+    reps, shards = sizes["rep"], sizes["shard"]
+    width, units = args[2].shape[2], args[3].shape[2]
+    even = H % reps == 0 and shards % 2 == 0 and shards > 2 and reps > 1
+    if args[1].shape[0] == 1 and args[0].shape[0] == 1 and even and units % (reps * shards) == 0:
+        if width // reps * reps == width:
+            return split_body(sizes, *args)
+    return body(*args)
+
+
 def solution(mesh):
+    sizes = {axis: mesh.shape[axis] for axis in ("rep", "shard")}
     in_specs = (
         P("shard", "rep", None),
         P(None, "shard", None),
@@ -276,4 +557,10 @@
         P(None, None, "shard"),
         P(None, "shard"),
     )
-    return jax.shard_map(body, mesh=mesh, in_specs=in_specs, out_specs=out_specs, check_vma=False)
+    return jax.shard_map(
+        functools.partial(run, sizes),
+        mesh=mesh,
+        in_specs=in_specs,
+        out_specs=out_specs,
+        check_vma=False,
+    )

time: 606 us -> 283 us (0.47)
  waiting for transfers between devices: 363 us -> 0.78 us
  Pallas kernels: 0 us -> 158 us
  blocking collectives: 95.3 us -> 0 us
  matrix products: 78.3 us -> 48.4 us
  other arithmetic: 11.4 us -> 18.1 us
    reduce_scatter x4 -> x1, waiting for transfers between devices: 170 us -> 0.01 us  [split_body(): lax.psum_scatter(jnp.concatenate([d_up.astype(BF16), d_down.astype(BF16)]...]
    pallas_call x0 -> x8, Pallas kernels: none -> 158 us  [exchange(): pl.pallas_call(functools.partial(exchange_body, plan, sizes), out_shape=s...]
    unnamed x17 -> x4, waiting for transfers between devices: 77.4 us -> 0.73 us
    all_gather x5 -> x0, blocking collectives: 71.4 us -> none  [the longest x1 16.9 us: body(): lax.all_gather(biases[layer], 'shard', axis=1, tiled=True)]
    all_gather x4 -> x3, waiting for transfers between devices: 62.9 us -> 0.04 us  [the longest x1 0.02 us: split_body(): w_up = lax.all_gather(w_up_part, 'shard', axis=0, tiled=True)]
    psum x1 -> x0, waiting for transfers between devices: 53.3 us -> none  [body(): lax.psum(owned[0].astype(jnp.bfloat16), 'rep').astype(jnp.float32)]
    dot_general x10 -> x11, matrix products: 51.9 us -> 33.8 us  [the longest x1 6.62 us: split_body(): pre = jnp.dot(c_low, w_up, preferred_element_type=F32) + up_bias]
    slice x3 -> x12, local copies, waits for them, and re-layouts: 17.9 us -> 3.58 us  [the longest x2 1.48 us: split_body(): g_attn_in = attn_all[:, :, :3 * cols].reshape(reps, part, 3, cols)]
  transfers between devices with their start and end apart: 13 -> 4, of which waited for: 11 -> 0; matrix products, arithmetic and copies ran while one was open for 15% -> 28% of each run, Pallas kernels for 0% -> 42%
where the time goes in v1:
time: 283 us; the launch traced here: 282 us
  Pallas kernels  158 us (56%)
  matrix products  48.4 us (17%)
  local copies, waits for them, and re-layouts  41.5 us (15%)
  other arithmetic  18.1 us (6%)
  between operations  14.5 us (5%)
    pallas_call x8, Pallas kernels, exchange(): pl.pallas_call(functools.partial(exchange_body, plan, sizes), out_shape=s...  158 us
    dot_general x4, matrix products, contract_cols(): lax.dot_general(left, right, (((1,), (1,)), ((), ())), preferred_element_...  9.92 us
    dot_general x1, matrix products, split_body(): pre = jnp.dot(c_low, w_up, preferred_element_type=F32) + up_bias  6.62 us
    dot_general x1, matrix products, split_body(): jnp.einsum('hqk,qhd->khd', dscores, queries, preferred_element_type=F32)  6.35 us
    dot_general x1, matrix products, split_body(): jnp.einsum('hqk,khd->qhd', dscores, keys, preferred_element_type=F32)  6.31 us
  transfers between devices with their start and end apart: 4, of which 0 were waited for; matrix products, arithmetic and copies ran while one was open for 28% of the time, Pallas kernels for 42%

profile of v1, /device:TPU:0, one launch (start us, length us, event | category | flops | bytes accessed | tf_op | source)
XLA Modules:
  0.0 281.7 jit_solution(6531669285426286303)
XLA Ops:
  8.0 2.4 reshape_squeeze.27
  16.9 29.3 %shard_map.160 = (bf16[8,96,576]{2,1,0:T(8,128)(2,1)}, bf16[8,1,1152]{2,1,0:T(2,128)(2,1)}, bf16[4,128,768]{2,1,0:T(8,128)(2,1)}, bf16[4,128,768]{2,1,0:T(8,128)(2,1)}) custom-call(bf16[96,576]{1,0:T(8,128)(2,1)} %copy.47.refs_0_, bf16[1,1152]{1,0:T(2,128)(2,1)} %concatenate.13.refs_1_, bf16[128,768]{1,0:T(8,128)(2,1)} %bitcast.118, ...), custom_call_target="tpu_custom_call" | custom-call | tf_op jit(solution)/shard_map/pallas_call | solution.py:339
  48.0 1.4 convert_reduce_fusion.4
  56.1 16.8 %shard_map.161 = bf16[4,512,192]{2,1,0:T(8,128)(2,1)} custom-call(bf16[512,192]{1,0:T(8,128)(2,1)} %copy.49.refs_0_), custom_call_target="tpu_custom_call" | custom-call | tf_op jit(solution)/shard_map/pallas_call | solution.py:339
  74.1 1.6 copy.55
  75.8 1.7 fusion.84
  78.6 13.9 %shard_map.162 = bf16[4,128,768]{2,1,0:T(8,128)(2,1)} custom-call(bf16[128,768]{1,0:T(8,128)(2,1)} %add_convert_fusion.refs_0_), custom_call_target="tpu_custom_call" | custom-call | tf_op jit(solution)/shard_map/pallas_call | solution.py:339
  92.5 6.6 %fusion.23 = (bf16[512,768]{1,0:T(8,128)(2,1)S(1)}, f32[512,768]{1,0:T(8,128)}) fusion(f32[768]{0:T(1024)S(1)} %add.172, bf16[512,768]{1,0:T(8,128)(2,1)} %bitcast.142, bf16[768,768]{1,0:T(8,128)(2,1)} %all-gather.6.cloned.1.call-done), kind=kOutput, calls=%fused_computation.31 | convolution fusion | flops 629932032 | bytes 4328448 | tf_op jit(solution)/shard_map/dot_general | solution.py:426
  100.0 1.8 convolution_convert_fusion
  101.8 4.0 %fusion.85 = (f32[768]{0:T(1024)S(1)}, bf16[512,768]{1,0:T(8,128)(2,1)}) fusion(f32[512,768]{1,0:T(8,128)} %get-tuple-element.67, bf16[512,768]{1,0:T(8,128)(2,1)} %bitcast.156, bf16[1,768,768]{2,1,0:T(8,128)(2,1)} %all-gather.10.cloned.1.call-done), kind=kOutput, calls=%fused_computation.154 | convolution fusion | flops 608304384 | bytes 4328448 | tf_op jit(solution)/shard_map/dot_general | solution.py:50
  106.6 2.3 convolution_convert_fusion.1
  108.8 1.6 pad_maximum_fusion
  110.5 3.3 %convolution_convert_fusion.3 = bf16[512,768]{1,0:T(8,128)(2,1)} fusion(bf16[512,768]{1,0:T(8,128)(2,1)} %copy-done.34, bf16[1,768,768]{2,1,0:T(8,128)(2,1)} %all-gather.10.cloned.1.call-done), kind=kOutput, calls=%fused_computation.55 | convolution fusion | flops 604372992 | bytes 2752512 | tf_op jit(solution)/shard_map/dot_general | solution.py:428
  113.8 1.7 convolution_convert_fusion.4
  115.5 21.6 %shard_map.163 = (bf16[4,128,768]{2,1,0:T(8,128)(2,1)}, bf16[4,128,768]{2,1,0:T(8,128)(2,1)}) custom-call(bf16[4,128,768]{2,1,0:T(8,128)(2,1)} %bitcast.141, bf16[4,128,768]{2,1,0:T(8,128)(2,1)} %bitcast.140), custom_call_target="tpu_custom_call" | custom-call | tf_op jit(solution)/shard_map/pallas_call | solution.py:339
  137.2 1.5 convert_reduce_fusion.2
  143.8 12.1 %shard_map.164 = bf16[4,128,768]{2,1,0:T(8,128)(2,1)} custom-call(bf16[128,768]{1,0:T(8,128)(2,1)} %convert_element_type.133.refs_0_), custom_call_target="tpu_custom_call" | custom-call | tf_op jit(solution)/shard_map/pallas_call | solution.py:339
  156.0 1.8 copy.56
  160.3 3.2 %fusion.89 = f32[3,512,512]{1,2,0:T(8,128)} fusion(bf16[512,3,64]{0,2,1:T(8,128)(2,1)S(1)} %bitcast.127, bf16[512,3,64]{0,2,1:T(8,128)(2,1)} %bitcast.130), kind=kOutput, calls=%fused_computation.156 | convolution fusion | flops 100663296 | bytes 3538944 | tf_op jit(solution)/shard_map/qhd,khd->hqk/dot_general | solution.py:462
  163.5 6.3 %fusion.34 = f32[512,3,64]{0,2,1:T(8,128)S(1)} fusion(bf16[512,3,64]{0,2,1:T(8,128)(2,1)S(1)} %bitcast.139, f32[3,512,512]{1,2,0:T(8,128)} %fusion.89, f32[3,512]{1,0:T(4,128)S(1)} %log_add_fusion, f32[3,512,512]{1,2,0:T(8,128)} %copy-done.1), kind=kOutput, calls=%fused_computation.59 | convolution fusion | flops 107743232 | bytes 6887424 | tf_op jit(solution)/shard_map/hqk,khd->qhd/dot_general | solution.py:465
  169.8 2.7 fusion.82
  173.0 6.3 %fusion.44 = bf16[512,1,3,64]{0,3,2,1:T(8,128)(2,1)S(1)} fusion(bf16[512,3,64]{0,2,1:T(8,128)(2,1)S(1)} %bitcast.135, f32[3,512,512]{1,2,0:T(8,128)} %fusion.89, f32[3,512]{1,0:T(4,128)S(1)} %log_add_fusion, f32[3,512,512]{1,2,0:T(8,128)} %copy-done.1), kind=kOutput, calls=%fused_computation.70 | convolution fusion | flops 107841536 | bytes 6690816 | tf_op jit(solution)/shard_map/hqk,qhd->khd/dot_general | solution.py:466
  179.4 1.6 convolution_convert_fusion.6
  181.8 1.7 copy.57
  183.5 2.9 %convolution_convert_fusion.5 = bf16[512,768]{1,0:T(8,128)(2,1)} fusion(bf16[512,576]{0,1:T(8,128)(2,1)S(1)} %bitcast.147, bf16[768,576]{1,0:T(8,128)(2,1)} %bitcast.132), kind=kOutput, calls=%fused_computation.57 | convolution fusion | flops 453378048 | bytes 2260992 | tf_op jit(solution)/shard_map/dot_general | solution.py:50
  186.5 25.7 %shard_map.165 = (bf16[4,128,768]{2,1,0:T(8,128)(2,1)}, bf16[8,96,768]{2,1,0:T(8,128)(2,1)}) custom-call(bf16[4,128,768]{2,1,0:T(8,128)(2,1)} %bitcast.144, bf16[8,96,768]{2,1,0:T(8,128)(2,1)} %bitcast.122), custom_call_target="tpu_custom_call" | custom-call | tf_op jit(solution)/shard_map/pallas_call | solution.py:339
  212.2 1.6 convert_reduce_fusion
  216.8 33.0 %shard_map.166 = (bf16[4,96,1536]{2,1,0:T(8,128)(2,1)}, bf16[4,96,768]{2,1,0:T(8,128)(2,1)}, f32[8,1,1152]{2,1,0:T(1,128)}) custom-call(bf16[96,1536]{1,0:T(8,128)(2,1)} %reduce-scatter.2.cloned.1.call-done.refs_0_, bf16[96,768]{1,0:T(8,128)(2,1)} %reduce_sum.265.refs_1_, f32[8,1,1152]{2,1,0:T(1,128)} %broadcast_in_dim.11.refs_2_), custom_call_target="tpu_custom_call" | custom-call | tf_op jit(solution)/shard_map/pallas_call | solution.py:339
  251.2 5.9 %shard_map.167 = f32[4,1,1152]{2,1,0:T(1,128)} custom-call(f32[1,1152]{1,0:T(1,128)} %reduce_sum.276.refs_0_), custom_call_target="tpu_custom_call" | custom-call | tf_op jit(solution)/shard_map/pallas_call | solution.py:339
  263.3 1.7 broadcast_in_dim_reshape.21
  269.4 2.2 copy.63
  271.6 3.6 %broadcast_in_dim_reshape.23 = f32[1,96,3072]{2,1,0:T(8,128)} reshape(f32[96,8,4,96]{3,2,1,0:T(4,128)} %copy.63) | data formatting | bytes 2359296 | tf_op jit(solution)/shard_map/broadcast_in_dim;reshape | solution.py:518
  (194 shorter events, 43.4 us)
Async XLA Ops:
  7.2 5.4 %copy-start = (bf16[1,384,768]{2,1,0:T(8,128)(2,1)S(1)}, bf16[1,384,768]{2,1,0:T(8,128)(2,1)}, u32[]{:S(2)}) copy-start(bf16[1,384,768]{2,1,0:T(8,128)(2,1)} %param.13) | copy-start | bytes 1769476
  7.2 6.1 %copy-start.4 = (bf16[1,128,768]{2,1,0:T(8,128)(2,1)S(1)}, bf16[1,128,768]{2,1,0:T(8,128)(2,1)}, u32[]{:S(2)}) copy-start(bf16[1,128,768]{2,1,0:T(8,128)(2,1)} %param.9) | copy-start | bytes 589828
  7.2 68.6 %all-gather.8.cloned.1.call-start = ((), (), s32[]{:S(2)}) async-start(), calls=%async_computation.3 | async-start | bytes 1327104 | tf_op jit(solution)/shard_map/all_gather | solution.py:382
  7.9 5.5 %copy-start.33 = (bf16[1,2,96]{2,1,0:T(2,128)(2,1)S(1)}, bf16[1,2,96]{2,1,0:T(2,128)(2,1)}, u32[]{:S(2)}) copy-start(bf16[1,2,96]{2,1,0:T(2,128)(2,1)} %param.14) | copy-start | bytes 1156
  7.9 5.6 %copy-start.29 = (bf16[1,6,96]{2,1,0:T(8,128)(2,1)S(1)}, bf16[1,6,96]{2,1,0:T(8,128)(2,1)}, u32[]{:S(2)}) copy-start(bf16[1,6,96]{2,1,0:T(8,128)(2,1)} %param.15) | copy-start | bytes 3460
  8.0 5.7 %copy-start.11 = (f32[1,128,768]{2,1,0:T(8,128)S(1)}, f32[1,128,768]{2,1,0:T(8,128)}, u32[]{:S(2)}) copy-start(f32[1,128,768]{2,1,0:T(8,128)} %param.17) | copy-start | bytes 1179652
  8.0 84.5 %all-gather.6.cloned.1.call-start = ((), (), s32[]{:S(2)}) async-start(), calls=%async_computation.1 | async-start | bytes 1327104 | tf_op jit(solution)/shard_map/all_gather | solution.py:383
  8.0 6.3 %copy-start.21 = (bf16[1,96,2304]{2,1,0:T(8,128)(2,1)S(1)}, bf16[1,96,2304]{2,1,0:T(8,128)(2,1)}, u32[]{:S(2)}) copy-start(bf16[1,96,2304]{2,1,0:T(8,128)(2,1)} %param.10) | copy-start | bytes 1327108
  12.5 89.3 %all-gather.10.cloned.1.call-start = ((), (), s32[]{:S(2)}) async-start(), calls=%async_computation.4 | async-start | bytes 1327104 | tf_op jit(solution)/shard_map/all_gather | solution.py:384
  13.3 3.0 %copy-start.30 = (bf16[1,384]{1,0:T(2,128)(2,1)S(1)}, bf16[1,384]{1,0:T(2,128)(2,1)}, u32[]{:S(2)}) copy-start(bf16[1,384]{1,0:T(2,128)(2,1)} %param.16) | copy-start | bytes 2308
  13.3 203.5 %reduce-scatter.2.cloned.1.call-start = ((), (), s32[]{:S(2)}) async-start(), calls=%async_computation.2 | async-start | bytes 2654208 | tf_op jit(solution)/shard_map/reduce_scatter | solution.py:436
  14.4 32.8 %copy-start.5 = (bf16[1,128,768]{2,1,0:T(8,128)(2,1)S(1)}, bf16[1,128,768]{2,1,0:T(8,128)(2,1)}, u32[]{:S(2)}) copy-start(bf16[1,128,768]{2,1,0:T(8,128)(2,1)} %param.9) | copy-start | bytes 589828
  46.2 3.2 %copy-start.2 = (bf16[4,128,768]{2,1,0:T(8,128)(2,1)S(1)}, bf16[4,128,768]{2,1,0:T(8,128)(2,1)}, u32[]{:S(2)}) copy-start(bf16[4,128,768]{2,1,0:T(8,128)(2,1)} %get-tuple-element.20) | copy-start | bytes 2359300
  47.2 2.6 copy-start.26
  48.0 3.2 %copy-start.14 = (bf16[8,96,576]{2,1,0:T(8,128)(2,1)S(1)}, bf16[8,96,576]{2,1,0:T(8,128)(2,1)}, u32[]{:S(2)}) copy-start(bf16[8,96,576]{2,1,0:T(8,128)(2,1)} %get-tuple-element.22) | copy-start | bytes 2654212
  92.5 7.5 %copy-start.32 = (bf16[4,128,768]{2,1,0:T(8,128)(2,1)S(1)}, bf16[4,128,768]{2,1,0:T(8,128)(2,1)}, u32[]{:S(2)}) copy-start(bf16[4,128,768]{2,1,0:T(8,128)(2,1)} %get-tuple-element.23) | copy-start | bytes 2359300
  106.6 2.3 copy-start.13
  110.5 3.3 %copy-start.31 = (bf16[768,768]{1,0:T(8,128)(2,1)S(1)}, bf16[768,768]{1,0:T(8,128)(2,1)}, u32[]{:S(2)}) copy-start(bf16[768,768]{1,0:T(8,128)(2,1)} %all-gather.6.cloned.1.call-done) | copy-start | bytes 3538948
  110.5 3.3 %copy-start.35 = (bf16[512,768]{1,0:T(8,128)(2,1)S(1)}, bf16[512,768]{1,0:T(8,128)(2,1)}, u32[]{:S(2)}) copy-start(bf16[512,768]{1,0:T(8,128)(2,1)} %get-tuple-element.69) | copy-start | bytes 2359300
  156.0 3.0 %copy-start.3 = (bf16[4,128,768]{2,1,0:T(8,128)(2,1)S(1)}, bf16[4,128,768]{2,1,0:T(8,128)(2,1)}, u32[]{:S(2)}) copy-start(bf16[4,128,768]{2,1,0:T(8,128)(2,1)} %shard_map.164) | copy-start | bytes 2359300
  160.3 3.2 %copy-start.18 = (bf16[512,192]{0,1:T(8,128)(2,1)S(1)}, bf16[512,192]{0,1:T(8,128)(2,1)}, u32[]{:S(2)}) copy-start(bf16[512,192]{0,1:T(8,128)(2,1)} %copy-done.17) | copy-start | bytes 589828
  169.8 3.1 %copy-start.16 = (bf16[512,192]{0,1:T(8,128)(2,1)S(1)}, bf16[512,192]{0,1:T(8,128)(2,1)}, u32[]{:S(2)}) copy-start(bf16[512,192]{0,1:T(8,128)(2,1)} %copy-done.15) | copy-start | bytes 589828
  181.8 1.7 copy-start.20
  186.4 27.4 %copy-start.27 = (f32[128]{0:T(128)S(1)}, f32[128]{0:T(128)}, u32[]{:S(2)}) copy-start(f32[128]{0:T(128)} %copy-done.26) | copy-start | bytes 1540
  186.4 27.4 %copy-start.28 = (f32[128]{0:T(128)S(1)}, f32[128]{0:T(128)}, u32[]{:S(2)}) copy-start(f32[128]{0:T(128)} %add_rsqrt_fusion.1) | copy-start | bytes 1540
  186.4 27.7 %copy-start.23 = (f32[1,8,96]{2,0,1:T(1,128)S(1)}, f32[1,8,96]{2,0,1:T(1,128)}, u32[]{:S(2)}) copy-start(f32[1,8,96]{2,0,1:T(1,128)} %stack.51) | copy-start | bytes 9220
  186.4 27.7 %copy-start.24 = (f32[1,8,96]{2,0,1:T(1,128)S(1)}, f32[1,8,96]{2,0,1:T(1,128)}, u32[]{:S(2)}) copy-start(f32[1,8,96]{2,0,1:T(1,128)} %stack.46) | copy-start | bytes 9220
  186.4 27.7 %copy-start.25 = (f32[1,8,96]{2,0,1:T(1,128)S(1)}, f32[1,8,96]{2,0,1:T(1,128)}, u32[]{:S(2)}) copy-start(f32[1,8,96]{2,0,1:T(1,128)} %stack.50) | copy-start | bytes 9220
  186.4 27.9 %copy-start.22 = (f32[8,384]{1,0:T(8,128)S(1)}, f32[8,384]{1,0:T(8,128)}, u32[]{:S(2)}) copy-start(f32[8,384]{1,0:T(8,128)} %reshape.299) | copy-start | bytes 36868
  212.2 2.8 %copy-start.12 = (bf16[8,96,768]{2,1,0:T(8,128)(2,1)S(1)}, bf16[8,96,768]{2,1,0:T(8,128)(2,1)}, u32[]{:S(2)}) copy-start(bf16[8,96,768]{2,1,0:T(8,128)(2,1)} %get-tuple-element.27) | copy-start | bytes 3538948
  249.8 9.9 %copy-start.7 = (bf16[4,96,768]{2,1,0:T(8,128)(2,1)S(1)}, bf16[4,96,768]{2,1,0:T(8,128)(2,1)}, u32[]{:S(2)}) copy-start(bf16[4,96,768]{2,1,0:T(8,128)(2,1)} %get-tuple-element.28) | copy-start | bytes 1769476
  265.0 2.5 copy-start.6
  (8 other events, 9.5 us)
Sparse Core Ops, SparseCore 0:
  9.7 34.2 all-gather.7
  46.1 22.8 all-gather.5
  71.3 22.2 all-gather.9
  110.6 36.7 reduce-scatter.1

commit v2 on v1

--- a/solution.py
+++ b/solution.py
@@ -266,13 +266,25 @@
     me = {axis: lax.axis_index(axis) for axis in sizes}
     barrier = pltpu.get_barrier_semaphore()
     greeted = 0
-    for axis in sorted({axis for axis, _ in plan}):
-        for step in range(1, sizes[axis]):
-            peer = lax.rem(me[axis] + step, sizes[axis])
-            pl.semaphore_signal(
-                barrier, inc=1, device_id={axis: peer}, device_id_type=pl.DeviceIdType.MESH
-            )
-            greeted += 1
+    offsets = set()
+    for axis, kind in plan:
+        for rep_step in range(sizes["rep"]):
+            for shard_step in range(sizes["shard"]):
+                along = (shard_step if axis == "rep" else rep_step) == 0
+                if (along or kind == "spread") and (rep_step, shard_step) != (0, 0):
+                    offsets.add((rep_step, shard_step))
+
+    def at(rep_step, shard_step):
+        return {
+            "rep": lax.rem(me["rep"] + rep_step, sizes["rep"]),
+            "shard": lax.rem(me["shard"] + shard_step, sizes["shard"]),
+        }
+
+    for offset in sorted(offsets):
+        pl.semaphore_signal(
+            barrier, inc=1, device_id=at(*offset), device_id_type=pl.DeviceIdType.MESH
+        )
+        greeted += 1
     pl.semaphore_wait(barrier, greeted)
 
     def copy(item, slot, source, target, axis, peer):
@@ -281,7 +293,7 @@
             dst_ref=target,
             send_sem=send_sem.at[item, slot],
             recv_sem=recv_sem.at[item, slot],
-            device_id={axis: peer},
+            device_id=peer if axis is None else {axis: peer},
             device_id_type=pl.DeviceIdType.MESH,
         )
 
@@ -303,6 +315,16 @@
             own = copy(item, 0, ins[item], outs[item].at[me[axis]], axis, sibling)
             own.start()
             copies.append(own)
+        elif kind == "spread":
+            for rep_step in range(sizes["rep"]):
+                for shard_step in range(sizes["shard"]):
+                    if (rep_step, shard_step) != (0, 0):
+                        peer = at(rep_step, shard_step)
+                        target = outs[item].at[me["rep"], me["shard"]]
+                        slot = rep_step * sizes["shard"] + shard_step
+                        one = copy(item, slot, ins[item].at[peer["shard"]], target, None, peer)
+                        one.start()
+                        copies.append(one)
         else:
             for step in range(1, size):
                 peer = lax.rem(me[axis] + step, size)
@@ -313,6 +335,8 @@
     for item, (axis, kind) in enumerate(plan):
         if kind == "swap":
             outs[item][me[axis]] = ins[item][me[axis]]
+        elif kind == "spread":
+            outs[item][me["rep"], me["shard"]] = ins[item][me["shard"]]
         else:
             outs[item][me[axis]] = ins[item][...]
     for item, step, first, axis, sibling, origin in relays:
@@ -333,8 +357,12 @@
     shapes = []
     for array, axis, kind in items:
         shape = array.shape if kind == "swap" else (sizes[axis],) + array.shape
+        if kind == "spread":
+            shape = (sizes["rep"],) + array.shape
         shapes.append(jax.ShapeDtypeStruct(shape, array.dtype))
     slots = max(sizes[axis] for axis, _ in plan)
+    if any(kind == "spread" for _, kind in plan):
+        slots = sizes["rep"] * sizes["shard"]
     vmem = pl.BlockSpec(memory_space=pltpu.VMEM)
     return pl.pallas_call(
         functools.partial(exchange_body, plan, sizes),
@@ -347,6 +375,90 @@
         ],
         compiler_params=pltpu.CompilerParams(collective_id=number, has_side_effects=True),
     )(*arrays)
+
+
+def local(kernel, shapes, *arrays):
+    vmem = pl.BlockSpec(memory_space=pltpu.VMEM)
+    return pl.pallas_call(
+        kernel,
+        out_shape=shapes,
+        in_specs=[vmem] * len(arrays),
+        out_specs=[vmem] * len(shapes),
+    )(*arrays)
+
+
+def prepare_kernel(reps, shards, attn_in, fc_in, fc_out, w_in, w_ff):
+    rank = lax.axis_index("rep")
+    cols = w_in.shape[1] // 3
+    piece = fc_out.shape[0] // reps
+    width = cols * reps
+    share = shards * piece
+    for r in range(reps):
+
+        @pl.when(rank == r)
+        def _(r=r):
+            for k in range(3):
+                base = k * width + r * cols
+                w_in[:, k * cols : (k + 1) * cols] = attn_in[:, base : base + cols]
+            for k in range(shards):
+                base = (k * reps + r) * piece
+                w_ff[:, k * piece : (k + 1) * piece] = fc_in[:, base : base + piece]
+            w_ff[:, share:] = fc_out[r * piece : (r + 1) * piece, :]
+
+
+def finish_kernel(reps, shards, attn_all, ff_all, attn_in, attn_out, fc_in, fc_out):
+    width = attn_out.shape[1]
+    cols = width // reps
+    piece = fc_out.shape[0] // reps
+    share = shards * piece
+    for r in range(reps):
+        for k in range(3):
+            base = k * width + r * cols
+            attn_in[:, base : base + cols] = attn_all[r, :, k * cols : (k + 1) * cols].astype(F32)
+        attn_out[:, r * cols : (r + 1) * cols] = attn_all[r, :, 3 * cols :].astype(F32)
+        for k in range(shards):
+            base = (k * reps + r) * piece
+            fc_in[:, base : base + piece] = ff_all[r, :, k * piece : (k + 1) * piece].astype(F32)
+        fc_out[r * piece : (r + 1) * piece, :] = ff_all[r, :, share:].astype(F32)
+
+
+def attend_kernel(heads, qkv, mixed, lse):
+    cols = mixed.shape[1]
+    depth = cols // heads
+    scale = depth ** (-0.5)
+    for h in range(heads):
+        here = slice(h * depth, (h + 1) * depth)
+        query = qkv[:, h * depth : (h + 1) * depth]
+        key = qkv[:, cols + h * depth : cols + (h + 1) * depth]
+        value = qkv[:, 2 * cols + h * depth : 2 * cols + (h + 1) * depth]
+        scores = contract_cols(query, key) * scale
+        top = jnp.max(scores, axis=-1, keepdims=True)
+        total = top + jnp.log(jnp.sum(jnp.exp(scores - top), axis=-1, keepdims=True))
+        probs = jnp.exp(scores - total).astype(BF16)
+        mixed[:, here] = jnp.dot(probs, value, preferred_element_type=F32).astype(BF16)
+        lse[:, h : h + 1] = total
+
+
+def attend_back_kernel(heads, qkv, upstream, lse, grad, query_sum, value_sum):
+    cols = upstream.shape[1]
+    depth = cols // heads
+    scale = depth ** (-0.5)
+    for h in range(heads):
+        first = slice(h * depth, (h + 1) * depth)
+        second = slice(cols + h * depth, cols + (h + 1) * depth)
+        third = slice(2 * cols + h * depth, 2 * cols + (h + 1) * depth)
+        query, key, value, above = qkv[:, first], qkv[:, second], qkv[:, third], upstream[:, first]
+        probs = jnp.exp(contract_cols(query, key) * scale - lse[:, h : h + 1])
+        dprobs = contract_cols(above, value)
+        delta = jnp.sum(probs * dprobs, axis=-1, keepdims=True)
+        dscores = (probs * (dprobs - delta) * scale).astype(BF16)
+        dquery = jnp.dot(dscores, key, preferred_element_type=F32)
+        dvalue = contract_rows(probs.astype(BF16), above)
+        grad[:, first] = dquery.astype(BF16)
+        grad[:, second] = contract_rows(dscores, query).astype(BF16)
+        grad[:, third] = dvalue.astype(BF16)
+        query_sum[:, first] = jnp.sum(dquery, axis=0, keepdims=True)
+        value_sum[:, first] = jnp.sum(dvalue, axis=0, keepdims=True)
 
 
 def flat(blocks):
@@ -366,31 +478,38 @@
     share = units // reps
     piece = fc_out.shape[1] // reps
     heads = H // reps
-    scale = (width // H) ** (-0.5)
 
     def mine(array, axis):
         return lax.dynamic_index_in_dim(array, rank, axis, keepdims=False)
 
     state = hidden_in[0].astype(F32)
     upstream = out_grad[0]
-    w_in_part = mine(attn_in[0].reshape(part, 3, reps, cols), 2).reshape(part, 3 * cols)
-    w_up_part = mine(fc_in[0].reshape(part, shards, reps, piece), 2).reshape(part, share)
-    w_down_part = mine(fc_out[0].reshape(reps, piece, width), 0)
+    w_in_part, w_ff_part = local(
+        functools.partial(prepare_kernel, reps, shards),
+        [
+            jax.ShapeDtypeStruct((part, 3 * cols), BF16),
+            jax.ShapeDtypeStruct((part, share + width), BF16),
+        ],
+        attn_in[0],
+        fc_in[0],
+        fc_out[0],
+    )
     small = jnp.concatenate(
         [norm_gains[0].reshape(1, -1), biases[0].reshape(1, -1), fc_in_bias[0].reshape(1, -1)], axis=1
     )
-    w_out = lax.all_gather(attn_out[0], "shard", axis=0, tiled=True)
-    w_up = lax.all_gather(w_up_part, "shard", axis=0, tiled=True)
-    w_down = lax.all_gather(w_down_part, "shard", axis=0, tiled=True)
-    w_in, small, x_all, dy_low = exchange(
+    w_in, w_out, small, x_all, dy_low = exchange(
         sizes,
         0,
         (w_in_part, "shard", "relay"),
+        (attn_out[0], "shard", "relay"),
         (small, "shard", "gather"),
         (hidden_in[0], "rep", "gather"),
         (upstream.astype(BF16), "rep", "gather"),
     )
-    w_in, x_all, dy_low = flat(w_in), flat(x_all), flat(dy_low)
+    w_ff_part, w_in = lax.optimization_barrier((w_ff_part, w_in))
+    w_ff = lax.all_gather(w_ff_part, "shard", axis=0, tiled=True)
+    w_up, w_down = w_ff[:, :share], w_ff[:, share:]
+    w_in, w_out, x_all, dy_low = flat(w_in), flat(w_out), flat(x_all), flat(dy_low)
     small = small[:, 0, :].astype(F32)
     gains = small[:, : 2 * part].reshape(shards, 2, part).swapaxes(0, 1).reshape(2, width)
     shifts = small[:, 2 * part : 8 * part].reshape(shards, 6, part).swapaxes(0, 1).reshape(6, width)
@@ -400,22 +519,18 @@
     a_low = normed_all.astype(BF16)
     _, normed1, inv1 = norm_forward(state, gains[0], shifts[0])
     qkv = jnp.dot(a_low, w_in, preferred_element_type=F32)
-
-    def heads_of(values):
-        return values.reshape(values.shape[0], heads, cols // heads)
-
-    queries = heads_of((qkv[:, :cols] + mine(shifts[1].reshape(reps, cols), 0)).astype(BF16))
-    keys = heads_of(qkv[:, cols : 2 * cols].astype(BF16))
-    values_in = heads_of(
-        (qkv[:, 2 * cols :] + mine(shifts[2].reshape(reps, cols), 0)).astype(BF16)
-    )
-    scores = jnp.einsum("qhd,khd->hqk", queries, keys, preferred_element_type=F32) * scale
-    top = jnp.max(scores, axis=-1, keepdims=True)
-    lse = top + jnp.log(jnp.sum(jnp.exp(scores - top), axis=-1, keepdims=True))
-    probs = jnp.exp(scores - lse)
-    weights = probs.astype(BF16)
-    attended = jnp.einsum("hqk,khd->qhd", weights, values_in, preferred_element_type=F32)
-    attended = attended.reshape(reps * rows, cols).astype(BF16)
+    query_bias = mine(shifts[1].reshape(reps, cols), 0)
+    value_bias = mine(shifts[2].reshape(reps, cols), 0)
+    qkv = qkv + jnp.concatenate([query_bias, jnp.zeros_like(query_bias), value_bias])
+    qkv = qkv.astype(BF16)
+    attended, lse = local(
+        functools.partial(attend_kernel, heads),
+        [
+            jax.ShapeDtypeStruct((reps * rows, cols), BF16),
+            jax.ShapeDtypeStruct((reps * rows, heads), F32),
+        ],
+        qkv,
+    )
     (o_all,) = exchange(sizes, 1, (attended, "rep", "gather"))
     o_rows = lax.dynamic_slice_in_dim(o_all, rank * rows, rows, 1)
     o_rows = o_rows.swapaxes(0, 1).reshape(rows, width)
@@ -439,13 +554,7 @@
         scatter_dimension=0,
         tiled=True,
     )
-    dmid_parts, y_parts = exchange(
-        sizes,
-        3,
-        (dmid_part.reshape(reps, rows, width), "rep", "swap"),
-        (y_part.reshape(reps, rows, width), "rep", "swap"),
-    )
-    result = mixed + jnp.sum(y_parts.astype(F32), axis=0) + shifts[5]
+    (dmid_parts,) = exchange(sizes, 3, (dmid_part.reshape(reps, rows, width), "rep", "swap"))
     dmid = jnp.sum(dmid_parts.astype(F32), axis=0)
     de5 = jnp.sum(upstream, axis=0)
     dmixed_part, dg2, de4 = norm_backward(dmid, gains[1], normed2, inv2)
@@ -454,30 +563,35 @@
     (dmixed_low,) = exchange(sizes, 4, (dmixed.astype(BF16), "rep", "gather"))
     dmixed_low = flat(dmixed_low)
     w_out_rows = mine(w_out.reshape(reps, cols, width), 0)
-    dattended = heads_of(contract_cols(dmixed_low, w_out_rows).astype(BF16))
+    dattended = contract_cols(dmixed_low, w_out_rows).astype(BF16)
     dmixed_cols = mine(dmixed_low.reshape(reps * rows, reps, cols), 1)
     d_out = jnp.einsum("rtc,td->rcd", o_all, dmixed_cols, preferred_element_type=F32)
     d_out = d_out.reshape(width, cols)
 
-    dprobs = jnp.einsum("qhd,khd->hqk", dattended, values_in, preferred_element_type=F32)
-    delta = jnp.sum(probs * dprobs, axis=-1, keepdims=True)
-    dscores = (probs * (dprobs - delta) * scale).astype(BF16)
-    dquery = jnp.einsum("hqk,khd->qhd", dscores, keys, preferred_element_type=F32)
-    dkey = jnp.einsum("hqk,qhd->khd", dscores, queries, preferred_element_type=F32)
-    dvalue = jnp.einsum("hqk,qhd->khd", weights, dattended, preferred_element_type=F32)
-    g_qkv = jnp.stack([dquery, dkey, dvalue], axis=1).reshape(reps * rows, 3 * cols)
-    de1 = jnp.sum(dquery, axis=0).reshape(cols)
-    de2 = jnp.sum(dvalue, axis=0).reshape(cols)
-    g_qkv = g_qkv.astype(BF16)
+    g_qkv, de1, de2 = local(
+        functools.partial(attend_back_kernel, heads),
+        [
+            jax.ShapeDtypeStruct((reps * rows, 3 * cols), BF16),
+            jax.ShapeDtypeStruct((1, cols), F32),
+            jax.ShapeDtypeStruct((1, cols), F32),
+        ],
+        qkv,
+        dattended,
+        lse,
+    )
+    de1, de2 = de1[0], de2[0]
     dnormed_part = contract_cols(g_qkv, w_in).astype(BF16)
     d_qkv = contract_rows(a_low, g_qkv)
     attn_grads = jnp.concatenate([d_qkv.astype(BF16), d_out.astype(BF16)], axis=1)
-    dnormed_parts, attn_parts = exchange(
+    dnormed_parts, y_parts, ff_all, attn_parts = exchange(
         sizes,
         5,
         (dnormed_part.reshape(reps, rows, width), "rep", "swap"),
+        (y_part.reshape(reps, rows, width), "rep", "swap"),
+        (ff_grads, "rep", "gather"),
         (attn_grads.reshape(shards, part, width), "shard", "swap"),
     )
+    result = mixed + jnp.sum(y_parts.astype(F32), axis=0) + shifts[5]
     attn_sum = jnp.sum(attn_parts.astype(F32), axis=0).astype(BF16)
     dnormed = jnp.sum(dnormed_parts.astype(F32), axis=0)
     dstate_part, dg1, de0 = norm_backward(dnormed, gains[0], normed1, inv1)
@@ -494,22 +608,21 @@
         jnp.zeros((shards, reps, piece), F32), bias_parts, rank, 1
     ).reshape(shards, reps * piece)
     vectors = jnp.concatenate([full, bias_parts], axis=1)[:, None, :]
-    ff_all, attn_all, vectors = exchange(
-        sizes,
-        6,
-        (ff_grads, "rep", "gather"),
-        (attn_sum, "rep", "gather"),
-        (vectors, "shard", "swap"),
-    )
-    (vectors,) = exchange(sizes, 7, (jnp.sum(vectors, axis=0), "rep", "gather"))
-    vectors = jnp.sum(vectors, axis=0).reshape(-1)
-    attn_all, ff_all = attn_all.astype(F32), ff_all.astype(F32)
-    g_attn_in = attn_all[:, :, : 3 * cols].reshape(reps, part, 3, cols)
-    g_attn_in = g_attn_in.transpose(1, 2, 0, 3).reshape(part, 3 * width)
-    g_attn_out = attn_all[:, :, 3 * cols :].swapaxes(0, 1).reshape(part, width)
-    g_fc_in = ff_all[:, :, :share].reshape(reps, part, shards, piece)
-    g_fc_in = g_fc_in.transpose(1, 2, 0, 3).reshape(part, units)
-    g_fc_out = ff_all[:, :, share:].reshape(reps * piece, width)
+    attn_all, vectors = exchange(
+        sizes, 6, (attn_sum, "rep", "gather"), (vectors, "shard", "spread")
+    )
+    vectors = jnp.sum(vectors, axis=(0, 1)).reshape(-1)
+    g_attn_in, g_attn_out, g_fc_in, g_fc_out = local(
+        functools.partial(finish_kernel, reps, shards),
+        [
+            jax.ShapeDtypeStruct((part, 3 * width), F32),
+            jax.ShapeDtypeStruct((part, width), F32),
+            jax.ShapeDtypeStruct((part, units), F32),
+            jax.ShapeDtypeStruct((reps * piece, width), F32),
+        ],
+        attn_all,
+        ff_all,
+    )
     return (
         result[None],
         dstate[None],

time: 283 us -> 234 us (0.83)
  matrix products: 48.4 us -> 23.2 us
  local copies, waits for them, and re-layouts: 41.5 us -> 18 us
  Pallas kernels: 158 us -> 161 us
    dot_general x6 -> x0, matrix products: 19.9 us -> none  [the longest x1 6.35 us: split_body(): jnp.einsum('hqk,qhd->khd', dscores, queries, preferred_element_type=F32)]
    pallas_call x0 -> x4, Pallas kernels: none -> 15.5 us  [local(): pl.pallas_call(kernel, out_shape=shapes, in_specs=[vmem] * len(arrays), o...]
    pallas_call x8 -> x7, Pallas kernels: 158 us -> 145 us  [exchange(): pl.pallas_call(functools.partial(exchange_body, plan, sizes), out_shape=s...]
    another operation x11 -> x4, local copies, waits for them, and re-layouts: 9.48 us -> 0.16 us  [the longest x1 0.08 us: split_body(): value_bias = mine(shifts[2].reshape(reps, cols), 0)]
    transpose x4 -> x0, local copies, waits for them, and re-layouts: 4.51 us -> none  [the longest x1 2.17 us: split_body(): g_fc_in = g_fc_in.transpose(1, 2, 0, 3).reshape(part, units)]
  transfers between devices with their start and end apart: 4 -> 2, of which waited for: 0 -> 0; matrix products, arithmetic and copies ran while one was open for 28% -> 14% of each run, Pallas kernels for 42% -> 28%
where the time goes in v2:
time: 234 us; the launch traced here: 233 us
  Pallas kernels  161 us (69%)
  matrix products  23.2 us (10%)
  local copies, waits for them, and re-layouts  18 us (8%)
  other arithmetic  16.4 us (7%)
  between operations  14.5 us (6%)
    pallas_call x7, Pallas kernels, exchange(): pl.pallas_call(functools.partial(exchange_body, plan, sizes), out_shape=s...  145 us
    pallas_call x4, Pallas kernels, local(): pl.pallas_call(kernel, out_shape=shapes, in_specs=[vmem] * len(arrays), o...  15.5 us
    dot_general x4, matrix products, contract_cols(): lax.dot_general(left, right, (((1,), (1,)), ((), ())), preferred_element_...  8.68 us
    dot_general x1, matrix products, split_body(): pre = jnp.dot(c_low, w_up, preferred_element_type=F32) + up_bias  5.67 us
  transfers between devices with their start and end apart: 2, of which 0 were waited for; matrix products, arithmetic and copies ran while one was open for 14% of the time, Pallas kernels for 28%

profile of v2, /device:TPU:0, one launch (start us, length us, event | category | flops | bytes accessed | tf_op | source)
XLA Modules:
  0.0 232.8 jit_solution(14270999857333549226)
XLA Ops:
  8.7 1.7 fusion.48
  10.4 1.4 concatenate.16.refs_2_
  11.8 2.3 shard_map.160
  14.1 34.6 %shard_map.161 = (bf16[8,96,576]{2,1,0:T(8,128)(2,1)}, bf16[8,96,768]{2,1,0:T(8,128)(2,1)}, bf16[8,1,1152]{2,1,0:T(2,128)(2,1)}, bf16[4,128,768]{2,1,0:T(8,128)(2,1)}, bf16[4,128,768]{2,1,0:T(8,128)(2,1)}) custom-call(bf16[96,576]{1,0:T(8,128)(2,1)} %get-tuple-element.33.refs_0_, bf16[96,768]{1,0:T(8,128)(2,1)} %bitcast.107, ...), custom_call_target="tpu_custom_call" | custom-call | tf_op jit(solution)/shard_map/pallas_call | solution.py:367
  50.8 1.4 convert_reduce_fusion.5
  52.9 1.6 fusion.19.qkv
  54.6 4.2 %shard_map.162 = (bf16[512,192]{1,0:T(8,128)(2,1)}, f32[512,3]{1,0:T(8,128)}) custom-call(bf16[512,576]{1,0:T(8,128)(2,1)} %fusion.19.qkv), custom_call_target="tpu_custom_call" | custom-call | tf_op jit(solution)/shard_map/pallas_call | solution.py:382
  58.7 16.7 %shard_map.163 = bf16[4,512,192]{2,1,0:T(8,128)(2,1)} custom-call(bf16[512,192]{1,0:T(8,128)(2,1)} %get-tuple-element.39.refs_0_), custom_call_target="tpu_custom_call" | custom-call | tf_op jit(solution)/shard_map/pallas_call | solution.py:367
  75.4 1.0 dynamic-slice_bitcast_fusion
  78.1 13.7 %shard_map.164 = bf16[4,128,768]{2,1,0:T(8,128)(2,1)} custom-call(bf16[128,768]{1,0:T(8,128)(2,1)} %add_convert_fusion.1.refs_0_), custom_call_target="tpu_custom_call" | custom-call | tf_op jit(solution)/shard_map/pallas_call | solution.py:367
  91.8 5.7 %fusion.7 = (bf16[512,768]{1,0:T(8,128)(2,1)S(1)}, f32[512,768]{1,0:T(8,128)S(1)}) fusion(f32[768]{0:T(1024)S(1)} %add.146, bf16[512,768]{1,0:T(8,128)(2,1)} %bitcast.98, bf16[768,1536]{1,0:T(8,128)(2,1)} %all-gather.2.cloned.1.call-done), kind=kOutput, calls=%fused_computation.14 | convolution fusion | flops 629932032 | bytes 4328448 | tf_op jit(solution)/shard_map/dot_general | solution.py:541
  97.5 1.1 fusion.50
  100.6 1.6 pad_maximum_fusion
  102.4 1.0 copy-done.3
  103.4 1.2 copy.36
  105.0 1.3 fusion.11
  106.7 3.0 %convolution_convert_fusion.4 = bf16[512,768]{1,0:T(8,128)(2,1)} fusion(bf16[768,1536]{1,0:T(8,128)(2,1)} %all-gather.2.cloned.1.call-done, bf16[512,768]{1,0:T(8,128)(2,1)S(1)} %copy-done.16), kind=kOutput, calls=%fused_computation.45 | convolution fusion | flops 604372992 | bytes 2752512 | tf_op jit(solution)/shard_map/dot_general | solution.py:50
  109.7 12.9 %shard_map.165 = bf16[4,128,768]{2,1,0:T(8,128)(2,1)} custom-call(bf16[4,128,768]{2,1,0:T(8,128)(2,1)} %bitcast.96), custom_call_target="tpu_custom_call" | custom-call | tf_op jit(solution)/shard_map/pallas_call | solution.py:367
  122.6 1.5 convert_reduce_fusion.2
  125.4 12.1 %shard_map.166 = bf16[4,128,768]{2,1,0:T(8,128)(2,1)} custom-call(bf16[128,768]{1,0:T(8,128)(2,1)} %convert_element_type.93.refs_0_), custom_call_target="tpu_custom_call" | custom-call | tf_op jit(solution)/shard_map/pallas_call | solution.py:367
  137.6 1.6 copy.37
  139.2 1.4 convolution_convert_fusion.7
  141.4 5.5 %shard_map.167 = (bf16[512,576]{1,0:T(8,128)(2,1)}, f32[1,192]{1,0:T(1,128)}, f32[1,192]{1,0:T(1,128)}) custom-call(bf16[512,576]{1,0:T(8,128)(2,1)} %fusion.19.qkv, bf16[512,192]{1,0:T(8,128)(2,1)} %copy.33.upstream, f32[512,3]{1,0:T(8,128)} %get-tuple-element.43.lse), custom_call_target="tpu_custom_call" | custom-call | tf_op jit(solution)/shard_map/pallas_call | solution.py:382
  149.2 2.0 convolution_convert_fusion.2
  151.3 1.5 copy.38
  152.8 3.2 %convolution_convert_fusion.5 = bf16[512,768]{1,0:T(8,128)(2,1)} fusion(bf16[512,576]{1,0:T(8,128)(2,1)} %get-tuple-element.44, bf16[768,576]{1,0:T(8,128)(2,1)} %bitcast.115), kind=kOutput, calls=%fused_computation.46 | convolution fusion | flops 453378048 | bytes 2260992 | tf_op jit(solution)/shard_map/dot_general | solution.py:50
  156.0 2.8 %convolution_convert_fusion.3 = bf16[512,768]{1,0:T(8,128)(2,1)} fusion(bf16[512,768]{1,0:T(8,128)(2,1)} %copy-done.14, bf16[768,1536]{1,0:T(8,128)(2,1)S(1)} %copy-done.11), kind=kOutput, calls=%fused_computation.44 | convolution fusion | flops 604372992 | bytes 2752512 | tf_op jit(solution)/shard_map/dot_general | solution.py:543
  158.8 40.3 %shard_map.168 = (bf16[4,128,768]{2,1,0:T(8,128)(2,1)}, bf16[4,128,768]{2,1,0:T(8,128)(2,1)}, bf16[4,96,1536]{2,1,0:T(8,128)(2,1)}, bf16[8,96,768]{2,1,0:T(8,128)(2,1)}) custom-call(bf16[4,128,768]{2,1,0:T(8,128)(2,1)} %bitcast.97, bf16[4,128,768]{2,1,0:T(8,128)(2,1)} %bitcast.100, bf16[96,1536]{1,0:T(8,128)(2,1)} %reduce-scatter.2.cloned.1.call-done.refs_2_, ...), custom_call_target="tpu_custom_call" | custom-call | tf_op jit(solution)/shard_map/pallas_call | solution.py:367
  199.2 1.6 convert_reduce_fusion
  202.8 14.8 %shard_map.169 = (bf16[4,96,768]{2,1,0:T(8,128)(2,1)}, f32[4,8,1,1152]{3,2,1,0:T(1,128)}) custom-call(bf16[96,768]{1,0:T(8,128)(2,1)} %reduce_sum.216.refs_0_, f32[8,1,1152]{2,1,0:T(1,128)} %broadcast_in_dim.43.refs_1_), custom_call_target="tpu_custom_call" | custom-call | tf_op jit(solution)/shard_map/pallas_call | solution.py:367
  217.6 1.0 reduce_sum.224
  222.4 3.5 %shard_map.170 = (f32[96,2304]{1,0:T(8,128)}, f32[96,768]{1,0:T(8,128)}, f32[96,3072]{1,0:T(8,128)}, f32[384,768]{1,0:T(8,128)}) custom-call(bf16[4,96,768]{2,1,0:T(8,128)(2,1)} %get-tuple-element.50.attn_all, bf16[4,96,1536]{2,1,0:T(8,128)(2,1)} %get-tuple-element.51.ff_all), custom_call_target="tpu_custom_call" | custom-call | tf_op jit(solution)/shard_map/pallas_call | solution.py:382
  (121 shorter events, 19.2 us)
Async XLA Ops:
  7.2 84.6 %all-gather.2.cloned.1.call-start = ((), (), s32[]{:S(2)}) async-start(), calls=%async_computation.1 | async-start | bytes 2654208 | tf_op jit(solution)/shard_map/all_gather | solution.py:510
  48.7 3.5 %copy-start = (bf16[4,128,768]{2,1,0:T(8,128)(2,1)S(1)}, bf16[4,128,768]{2,1,0:T(8,128)(2,1)}, u32[]{:S(2)}) copy-start(bf16[4,128,768]{2,1,0:T(8,128)(2,1)} %get-tuple-element.34) | copy-start | bytes 2359300
  48.7 110.1 %reduce-scatter.2.cloned.1.call-start = ((), (), s32[]{:S(2)}) async-start(), calls=%async_computation.2 | async-start | bytes 2654208 | tf_op jit(solution)/shard_map/reduce_scatter | solution.py:551
  50.8 2.2 copy-start.12
  54.6 22.0 %copy-start.2 = (bf16[1,128,768]{2,1,0:T(8,128)(2,1)S(1)}, bf16[1,128,768]{2,1,0:T(8,128)(2,1)}, u32[]{:S(2)}) copy-start(bf16[1,128,768]{2,1,0:T(8,128)(2,1)} %param.9) | copy-start | bytes 589828
  54.6 22.1 %copy-start.5 = (bf16[8,96,768]{2,1,0:T(8,128)(2,1)S(1)}, bf16[8,96,768]{2,1,0:T(8,128)(2,1)}, u32[]{:S(2)}) copy-start(bf16[8,96,768]{2,1,0:T(8,128)(2,1)} %get-tuple-element.40) | copy-start | bytes 3538948
  91.8 5.7 %copy-start.10 = (bf16[768,1536]{1,0:T(8,128)(2,1)S(1)}, bf16[768,1536]{1,0:T(8,128)(2,1)}, u32[]{:S(2)}) copy-start(bf16[768,1536]{1,0:T(8,128)(2,1)} %all-gather.2.cloned.1.call-done) | copy-start | bytes 7077892
  91.8 5.7 %copy-start.13 = (bf16[4,128,768]{2,1,0:T(8,128)(2,1)S(1)}, bf16[4,128,768]{2,1,0:T(8,128)(2,1)}, u32[]{:S(2)}) copy-start(bf16[4,128,768]{2,1,0:T(8,128)(2,1)} %get-tuple-element.41) | copy-start | bytes 2359300
  97.5 2.3 copy-start.14
  97.5 1.4 copy-start.9
  98.7 1.1 copy-start.15
  102.2 1.2 copy-start.3
  104.7 2.0 copy-start.16
  109.7 14.8 %copy-start.6 = (f32[1,128,768]{2,1,0:T(8,128)S(1)}, f32[1,128,768]{2,1,0:T(8,128)}, u32[]{:S(2)}) copy-start(f32[1,128,768]{2,1,0:T(8,128)} %param.17) | copy-start | bytes 1179652
  137.6 1.6 copy-start.1
  140.6 8.2 %copy-start.4 = (bf16[4,192,512]{2,1,0:T(8,128)(2,1)S(1)}, bf16[4,192,512]{2,1,0:T(8,128)(2,1)}, u32[]{:S(2)}) copy-start(bf16[4,192,512]{2,1,0:T(8,128)(2,1)} %copy.36) | copy-start | bytes 2359300
  152.8 3.3 %copy-start.11 = (bf16[768,1536]{1,0:T(8,128)(2,1)S(1)}, bf16[768,1536]{1,0:T(8,128)(2,1)}, u32[]{:S(2)}) copy-start(bf16[768,1536]{1,0:T(8,128)(2,1)} %all-gather.2.cloned.1.call-done) | copy-start | bytes 7077892
  199.2 2.8 %copy-start.7 = (bf16[8,96,768]{2,1,0:T(8,128)(2,1)S(1)}, bf16[8,96,768]{2,1,0:T(8,128)(2,1)}, u32[]{:S(2)}) copy-start(bf16[8,96,768]{2,1,0:T(8,128)(2,1)} %get-tuple-element.47) | copy-start | bytes 3538948
  200.7 18.5 %copy-start.8 = (bf16[4,128,768]{2,1,0:T(8,128)(2,1)S(1)}, bf16[4,128,768]{2,1,0:T(8,128)(2,1)}, u32[]{:S(2)}) copy-start(bf16[4,128,768]{2,1,0:T(8,128)(2,1)} %get-tuple-element.45) | copy-start | bytes 2359300
Sparse Core Ops, SparseCore 0:
  48.9 32.2 all-gather.1
  102.4 38.0 reduce-scatter.1

commit v3 on v2

--- a/solution.py
+++ b/solution.py
@@ -390,7 +390,7 @@
 def prepare_kernel(reps, shards, attn_in, fc_in, fc_out, w_in, w_ff):
     rank = lax.axis_index("rep")
     cols = w_in.shape[1] // 3
-    piece = fc_out.shape[0] // reps
+    piece = fc_out.shape[1] // reps
     width = cols * reps
     share = shards * piece
     for r in range(reps):
@@ -399,14 +399,14 @@
         def _(r=r):
             for k in range(3):
                 base = k * width + r * cols
-                w_in[:, k * cols : (k + 1) * cols] = attn_in[:, base : base + cols]
+                w_in[:, k * cols : (k + 1) * cols] = attn_in[0, :, base : base + cols]
             for k in range(shards):
                 base = (k * reps + r) * piece
-                w_ff[:, k * piece : (k + 1) * piece] = fc_in[:, base : base + piece]
-            w_ff[:, share:] = fc_out[r * piece : (r + 1) * piece, :]
-
-
-def finish_kernel(reps, shards, attn_all, ff_all, attn_in, attn_out, fc_in, fc_out):
+                w_ff[:, k * piece : (k + 1) * piece] = fc_in[0, :, base : base + piece]
+            w_ff[:, share:] = fc_out[0, r * piece : (r + 1) * piece, :]
+
+
+def finish_kernel(reps, shards, attn_all, out_all, ff_all, attn_in, attn_out, fc_in, fc_out):
     width = attn_out.shape[1]
     cols = width // reps
     piece = fc_out.shape[0] // reps
@@ -415,7 +415,7 @@
         for k in range(3):
             base = k * width + r * cols
             attn_in[:, base : base + cols] = attn_all[r, :, k * cols : (k + 1) * cols].astype(F32)
-        attn_out[:, r * cols : (r + 1) * cols] = attn_all[r, :, 3 * cols :].astype(F32)
+        attn_out[:, r * cols : (r + 1) * cols] = out_all[r].astype(F32)
         for k in range(shards):
             base = (k * reps + r) * piece
             fc_in[:, base : base + piece] = ff_all[r, :, k * piece : (k + 1) * piece].astype(F32)
@@ -490,30 +490,27 @@
             jax.ShapeDtypeStruct((part, 3 * cols), BF16),
             jax.ShapeDtypeStruct((part, share + width), BF16),
         ],
-        attn_in[0],
-        fc_in[0],
-        fc_out[0],
-    )
-    small = jnp.concatenate(
-        [norm_gains[0].reshape(1, -1), biases[0].reshape(1, -1), fc_in_bias[0].reshape(1, -1)], axis=1
-    )
-    w_in, w_out, small, x_all, dy_low = exchange(
+        attn_in,
+        fc_in,
+        fc_out,
+    )
+    w_in, gains, shifts, up_bias, x_all, dy_low = exchange(
         sizes,
         0,
         (w_in_part, "shard", "relay"),
-        (attn_out[0], "shard", "relay"),
-        (small, "shard", "gather"),
+        (norm_gains[0], "shard", "gather"),
+        (biases[0], "shard", "gather"),
+        (fc_in_bias, "shard", "gather"),
         (hidden_in[0], "rep", "gather"),
         (upstream.astype(BF16), "rep", "gather"),
     )
     w_ff_part, w_in = lax.optimization_barrier((w_ff_part, w_in))
     w_ff = lax.all_gather(w_ff_part, "shard", axis=0, tiled=True)
     w_up, w_down = w_ff[:, :share], w_ff[:, share:]
-    w_in, w_out, x_all, dy_low = flat(w_in), flat(w_out), flat(x_all), flat(dy_low)
-    small = small[:, 0, :].astype(F32)
-    gains = small[:, : 2 * part].reshape(shards, 2, part).swapaxes(0, 1).reshape(2, width)
-    shifts = small[:, 2 * part : 8 * part].reshape(shards, 6, part).swapaxes(0, 1).reshape(6, width)
-    up_bias = mine(small[:, 8 * part :].reshape(shards, reps, piece), 1).reshape(share)
+    w_in, x_all, dy_low = flat(w_in), flat(x_all), flat(dy_low)
+    gains = gains.astype(F32).swapaxes(0, 1).reshape(2, width)
+    shifts = shifts.astype(F32).swapaxes(0, 1).reshape(6, width)
+    up_bias = mine(up_bias.astype(F32).reshape(shards, reps, piece), 1).reshape(share)
 
     normed_all, normed1_all, inv1_all = norm_forward(x_all.astype(F32), gains[0], shifts[0])
     a_low = normed_all.astype(BF16)
@@ -531,7 +528,10 @@
         ],
         qkv,
     )
-    (o_all,) = exchange(sizes, 1, (attended, "rep", "gather"))
+    w_out, o_all = exchange(
+        sizes, 1, (attn_out[0], "shard", "relay"), (attended, "rep", "gather")
+    )
+    w_out = flat(w_out)
     o_rows = lax.dynamic_slice_in_dim(o_all, rank * rows, rows, 1)
     o_rows = o_rows.swapaxes(0, 1).reshape(rows, width)
     mixed = state + jnp.dot(o_rows, w_out, preferred_element_type=F32) + shifts[3]
@@ -580,16 +580,17 @@
         lse,
     )
     de1, de2 = de1[0], de2[0]
+    ff_grads, g_qkv = lax.optimization_barrier((ff_grads, g_qkv))
+    ff_all = lax.all_gather(ff_grads, "rep", axis=0)
     dnormed_part = contract_cols(g_qkv, w_in).astype(BF16)
     d_qkv = contract_rows(a_low, g_qkv)
-    attn_grads = jnp.concatenate([d_qkv.astype(BF16), d_out.astype(BF16)], axis=1)
-    dnormed_parts, y_parts, ff_all, attn_parts = exchange(
+    d_out = lax.psum_scatter(d_out.astype(BF16), "shard", scatter_dimension=0, tiled=True)
+    dnormed_parts, y_parts, attn_parts = exchange(
         sizes,
         5,
         (dnormed_part.reshape(reps, rows, width), "rep", "swap"),
         (y_part.reshape(reps, rows, width), "rep", "swap"),
-        (ff_grads, "rep", "gather"),
-        (attn_grads.reshape(shards, part, width), "shard", "swap"),
+        (d_qkv.astype(BF16).reshape(shards, part, 3 * cols), "shard", "swap"),
     )
     result = mixed + jnp.sum(y_parts.astype(F32), axis=0) + shifts[5]
     attn_sum = jnp.sum(attn_parts.astype(F32), axis=0).astype(BF16)
@@ -608,8 +609,12 @@
         jnp.zeros((shards, reps, piece), F32), bias_parts, rank, 1
     ).reshape(shards, reps * piece)
     vectors = jnp.concatenate([full, bias_parts], axis=1)[:, None, :]
-    attn_all, vectors = exchange(
-        sizes, 6, (attn_sum, "rep", "gather"), (vectors, "shard", "spread")
+    attn_all, out_all, vectors = exchange(
+        sizes,
+        6,
+        (attn_sum, "rep", "gather"),
+        (d_out, "rep", "gather"),
+        (vectors, "shard", "spread"),
     )
     vectors = jnp.sum(vectors, axis=(0, 1)).reshape(-1)
     g_attn_in, g_attn_out, g_fc_in, g_fc_out = local(
@@ -621,6 +626,7 @@
             jax.ShapeDtypeStruct((reps * piece, width), F32),
         ],
         attn_all,
+        out_all,
         ff_all,
     )
     return (

time: 234 us -> 242 us (1.034)
  other arithmetic: 16.4 us -> 19.3 us
  matrix products: 23.2 us -> 25.8 us
    concatenate x2 -> x0, local copies, waits for them, and re-layouts: 2.82 us -> none  [the longest x1 1.45 us: split_body(): jnp.concatenate([d_qkv.astype(BF16), d_out.astype(BF16)], axis=1)]
  transfers between devices with their start and end apart: 2 -> 4, of which waited for: 0 -> 0; matrix products, arithmetic and copies ran while one was open for 14% -> 21% of each run, Pallas kernels for 28% -> 53%
where the time goes in v3:
time: 242 us; the launch traced here: 241 us
  Pallas kernels  162 us (67%)
  matrix products  25.8 us (11%)
  other arithmetic  19.3 us (8%)
  local copies, waits for them, and re-layouts  18.6 us (8%)
  between operations  14.3 us (6%)
    pallas_call x7, Pallas kernels, exchange(): pl.pallas_call(functools.partial(exchange_body, plan, sizes), out_shape=s...  147 us
    pallas_call x4, Pallas kernels, local(): pl.pallas_call(kernel, out_shape=shapes, in_specs=[vmem] * len(arrays), o...  15.6 us
    dot_general x4, matrix products, contract_cols(): lax.dot_general(left, right, (((1,), (1,)), ((), ())), preferred_element_...  8.93 us
    dot_general x1, matrix products, split_body(): pre = jnp.dot(c_low, w_up, preferred_element_type=F32) + up_bias  5.67 us
  transfers between devices with their start and end apart: 4, of which 0 were waited for; matrix products, arithmetic and copies ran while one was open for 21% of the time, Pallas kernels for 53%

profile of v3, /device:TPU:0, one launch (start us, length us, event | category | flops | bytes accessed | tf_op | source)
XLA Modules:
  0.0 240.9 jit_solution(11178744380487468104)
XLA Ops:
  7.2 1.7 fusion.48
  8.9 2.3 shard_map.160
  11.2 28.1 %shard_map.161 = (bf16[8,96,576]{2,1,0:T(8,128)(2,1)}, bf16[8,2,96]{2,1,0:T(2,128)(2,1)}, bf16[8,6,96]{2,1,0:T(8,128)(2,1)}, bf16[8,1,384]{2,1,0:T(2,128)(2,1)},...) custom-call(bf16[96,576]{1,0:T(8,128)(2,1)} %get-tuple-element.38.refs_0_, bf16[2,96]{1,0:T(2,128)(2,1)} %bitcast.107, ...), custom_call_target="tpu_custom_call" | custom-call | tf_op jit(solution)/shard_map/pallas_call | solution.py:367
  43.0 1.4 convert_reduce_fusion.5
  46.3 1.6 fusion.19.qkv
  48.0 4.1 %shard_map.162 = (bf16[512,192]{1,0:T(8,128)(2,1)}, f32[512,3]{1,0:T(8,128)}) custom-call(bf16[512,576]{1,0:T(8,128)(2,1)} %fusion.19.qkv), custom_call_target="tpu_custom_call" | custom-call | tf_op jit(solution)/shard_map/pallas_call | solution.py:382
  52.1 25.7 %shard_map.163 = (bf16[8,96,768]{2,1,0:T(8,128)(2,1)}, bf16[4,512,192]{2,1,0:T(8,128)(2,1)}) custom-call(bf16[96,768]{1,0:T(8,128)(2,1)} %bitcast.102, bf16[512,192]{1,0:T(8,128)(2,1)} %get-tuple-element.45.refs_1_), custom_call_target="tpu_custom_call" | custom-call | tf_op jit(solution)/shard_map/pallas_call | solution.py:367
  78.9 1.7 fusion.49
  81.7 14.3 %shard_map.164 = bf16[4,128,768]{2,1,0:T(8,128)(2,1)} custom-call(bf16[128,768]{1,0:T(8,128)(2,1)} %add_convert_fusion.1.refs_0_), custom_call_target="tpu_custom_call" | custom-call | tf_op jit(solution)/shard_map/pallas_call | solution.py:367
  96.1 5.7 %fusion.7 = (bf16[512,768]{1,0:T(8,128)(2,1)S(1)}, f32[512,768]{1,0:T(8,128)S(1)}) fusion(f32[768]{0:T(1024)S(1)} %add.148, bf16[512,768]{1,0:T(8,128)(2,1)} %bitcast.99, bf16[768,1536]{1,0:T(8,128)(2,1)} %all-gather.4.cloned.1.call-done), kind=kOutput, calls=%fused_computation.14 | convolution fusion | flops 629932032 | bytes 4328448 | tf_op jit(solution)/shard_map/dot_general | solution.py:541
  101.8 1.7 fusion.50
  105.4 2.5 %copy.44 = bf16[768,1536]{1,0:T(8,128)(2,1)} copy(bf16[768,1536]{0,1:T(8,128)(2,1)S(1)} %pad_maximum_fusion) | data formatting | bytes 4718592
  108.9 1.5 copy.40
  111.4 1.3 fusion.11
  112.7 3.0 %convolution_convert_fusion.4 = bf16[512,768]{1,0:T(8,128)(2,1)} fusion(bf16[768,1536]{1,0:T(8,128)(2,1)} %all-gather.4.cloned.1.call-done, bf16[512,768]{1,0:T(8,128)(2,1)S(1)} %copy-done.31), kind=kOutput, calls=%fused_computation.45 | convolution fusion | flops 604372992 | bytes 2752512 | tf_op jit(solution)/shard_map/dot_general | solution.py:50
  115.7 13.4 %shard_map.165 = bf16[4,128,768]{2,1,0:T(8,128)(2,1)} custom-call(bf16[4,128,768]{2,1,0:T(8,128)(2,1)} %bitcast.97), custom_call_target="tpu_custom_call" | custom-call | tf_op jit(solution)/shard_map/pallas_call | solution.py:367
  129.1 1.5 convert_reduce_fusion.2
  131.7 13.3 %shard_map.166 = bf16[4,128,768]{2,1,0:T(8,128)(2,1)} custom-call(bf16[128,768]{1,0:T(8,128)(2,1)} %convert_element_type.91.refs_0_), custom_call_target="tpu_custom_call" | custom-call | tf_op jit(solution)/shard_map/pallas_call | solution.py:367
  145.0 1.5 copy.41
  146.9 1.1 convolution_convert_fusion.6
  148.1 3.3 %convolution_convert_fusion.3 = bf16[512,768]{1,0:T(8,128)(2,1)} fusion(bf16[512,768]{1,0:T(8,128)(2,1)} %copy-done.29, bf16[768,1536]{1,0:T(8,128)(2,1)} %all-gather.4.cloned.1.call-done), kind=kOutput, calls=%fused_computation.44 | convolution fusion | flops 604372992 | bytes 2752512 | tf_op jit(solution)/shard_map/dot_general | solution.py:543
  151.4 1.4 convolution_convert_fusion.7
  154.1 5.5 %shard_map.167 = (bf16[512,576]{1,0:T(8,128)(2,1)}, f32[1,192]{1,0:T(1,128)}, f32[1,192]{1,0:T(1,128)}) custom-call(bf16[512,576]{1,0:T(8,128)(2,1)} %fusion.19.qkv, bf16[512,192]{1,0:T(8,128)(2,1)} %copy.38.upstream, f32[512,3]{1,0:T(8,128)} %get-tuple-element.51.lse), custom_call_target="tpu_custom_call" | custom-call | tf_op jit(solution)/shard_map/pallas_call | solution.py:382
  161.4 1.2 copy.45
  163.4 1.8 convolution_convert_fusion.2
  165.2 1.3 copy.39
  166.6 2.9 %convolution_convert_fusion.5 = bf16[512,768]{1,0:T(8,128)(2,1)} fusion(bf16[512,576]{1,0:T(8,128)(2,1)S(1)} %copy-done.28, bf16[768,576]{1,0:T(8,128)(2,1)} %bitcast.110), kind=kOutput, calls=%fused_computation.46 | convolution fusion | flops 453378048 | bytes 2260992 | tf_op jit(solution)/shard_map/dot_general | solution.py:50
  169.5 33.2 %shard_map.168 = (bf16[4,128,768]{2,1,0:T(8,128)(2,1)}, bf16[4,128,768]{2,1,0:T(8,128)(2,1)}, bf16[8,96,576]{2,1,0:T(8,128)(2,1)}) custom-call(bf16[4,128,768]{2,1,0:T(8,128)(2,1)} %bitcast.101, bf16[4,128,768]{2,1,0:T(8,128)(2,1)} %bitcast.98, bf16[8,96,576]{2,1,0:T(8,128)(2,1)} %bitcast.89), custom_call_target="tpu_custom_call" | custom-call | tf_op jit(solution)/shard_map/pallas_call | solution.py:367
  202.8 1.6 convert_reduce_fusion
  207.0 18.8 %shard_map.169 = (bf16[4,96,576]{2,1,0:T(8,128)(2,1)}, bf16[4,96,192]{2,1,0:T(8,128)(2,1)}, f32[4,8,1,1152]{3,2,1,0:T(1,128)}) custom-call(bf16[96,576]{1,0:T(8,128)(2,1)} %reduce_sum.216.refs_0_, bf16[96,192]{1,0:T(8,128)(2,1)} %reduce-scatter.5.cloned.1.call-done.refs_1_, f32[8,1,1152]{2,1,0:T(1,128)} %broadcast_in_dim.43.refs_2_), custom_call_target="tpu_custom_call" | custom-call | tf_op jit(solution)/shard_map/pallas_call | solution.py:367
  225.8 1.0 reduce_sum.224
  230.6 3.7 %shard_map.170 = (f32[96,2304]{1,0:T(8,128)}, f32[96,768]{1,0:T(8,128)}, f32[96,3072]{1,0:T(8,128)}, f32[384,768]{1,0:T(8,128)}) custom-call(bf16[4,96,576]{2,1,0:T(8,128)(2,1)} %get-tuple-element.59.attn_all, bf16[4,96,192]{2,1,0:T(8,128)(2,1)} %get-tuple-element.60.out_all, bf16[4,96,1536]{2,1,0:T(8,128)(2,1)} %bitcast.94), custom_call_target="tpu_custom_call" | custom-call | tf_op jit(solution)/shard_map/pallas_call | solution.py:382
  (153 shorter events, 23.4 us)
Async XLA Ops:
  7.2 88.9 %all-gather.4.cloned.1.call-start = ((), (), s32[]{:S(2)}) async-start(), calls=%async_computation.2 | async-start | bytes 2654208 | tf_op jit(solution)/shard_map/all_gather | solution.py:508
  39.3 5.7 %copy-start = (bf16[4,128,768]{2,1,0:T(8,128)(2,1)S(1)}, bf16[4,128,768]{2,1,0:T(8,128)(2,1)}, u32[]{:S(2)}) copy-start(bf16[4,128,768]{2,1,0:T(8,128)(2,1)} %get-tuple-element.39) | copy-start | bytes 2359300
  39.3 122.0 %reduce-scatter.7.cloned.1.call-start = ((), (), s32[]{:S(2)}) async-start(), calls=%async_computation.5 | async-start | bytes 2654208
  43.0 3.3 %copy-start.26 = (bf16[8,96,576]{2,1,0:T(8,128)(2,1)S(1)}, bf16[8,96,576]{2,1,0:T(8,128)(2,1)}, u32[]{:S(2)}) copy-start(bf16[8,96,576]{2,1,0:T(8,128)(2,1)} %get-tuple-element.44) | copy-start | bytes 2654212
  48.0 30.9 %copy-start.2 = (bf16[1,128,768]{2,1,0:T(8,128)(2,1)S(1)}, bf16[1,128,768]{2,1,0:T(8,128)(2,1)}, u32[]{:S(2)}) copy-start(bf16[1,128,768]{2,1,0:T(8,128)(2,1)} %param.9) | copy-start | bytes 589828
  80.6 21.1 %copy-start.11 = (f32[128]{0:T(128)}, f32[128]{0:T(128)S(1)}, u32[]{:S(2)}) copy-start(f32[128]{0:T(128)S(1)} %broadcast_multiply_fusion.6) | copy-start | bytes 1540
  80.9 20.9 %copy-start.18 = (f32[128]{0:T(128)}, f32[128]{0:T(128)S(1)}, u32[]{:S(2)}) copy-start(f32[128]{0:T(128)S(1)} %add_rsqrt_fusion.2) | copy-start | bytes 1540
  96.1 5.7 %copy-start.25 = (bf16[768,1536]{1,0:T(8,128)(2,1)S(1)}, bf16[768,1536]{1,0:T(8,128)(2,1)}, u32[]{:S(2)}) copy-start(bf16[768,1536]{1,0:T(8,128)(2,1)} %all-gather.4.cloned.1.call-done) | copy-start | bytes 7077892
  96.1 5.7 %copy-start.27 = (bf16[4,128,768]{2,1,0:T(8,128)(2,1)S(1)}, bf16[4,128,768]{2,1,0:T(8,128)(2,1)}, u32[]{:S(2)}) copy-start(bf16[4,128,768]{2,1,0:T(8,128)(2,1)} %get-tuple-element.48) | copy-start | bytes 2359300
  101.8 2.6 %copy-start.29 = (bf16[512,768]{1,0:T(8,128)(2,1)}, bf16[512,768]{1,0:T(8,128)(2,1)S(1)}, u32[]{:S(2)}) copy-start(bf16[512,768]{1,0:T(8,128)(2,1)S(1)} %get-tuple-element.95) | copy-start | bytes 2359300
  107.9 2.6 %copy-start.3 = (bf16[1,128,768]{2,1,0:T(8,128)(2,1)S(1)}, bf16[1,128,768]{2,1,0:T(8,128)(2,1)}, u32[]{:S(2)}) copy-start(bf16[1,128,768]{2,1,0:T(8,128)(2,1)} %param.9) | copy-start | bytes 589828
  107.9 3.5 %copy-start.13 = (f32[512]{0:T(512)S(1)}, f32[512]{0:T(512)}, u32[]{:S(2)}) copy-start(f32[512]{0:T(512)} %get-tuple-element.89) | copy-start | bytes 6148
  107.9 3.4 %copy-start.14 = (f32[512]{0:T(512)S(1)}, f32[512]{0:T(512)}, u32[]{:S(2)}) copy-start(f32[512]{0:T(512)} %get-tuple-element.91) | copy-start | bytes 6148
  107.9 99.0 %reduce-scatter.5.cloned.1.call-start = ((), (), s32[]{:S(2)}) async-start(), calls=%async_computation.3 | async-start | bytes 442368 | tf_op jit(solution)/shard_map/reduce_scatter | solution.py:587
  108.9 3.8 %copy-start.31 = (bf16[512,768]{1,0:T(8,128)(2,1)S(1)}, bf16[512,768]{1,0:T(8,128)(2,1)}, u32[]{:S(2)}) copy-start(bf16[512,768]{1,0:T(8,128)(2,1)} %copy-done.30) | copy-start | bytes 2359300
  110.6 5.1 %copy-start.15 = (f32[128]{0:T(128)}, f32[128]{0:T(128)S(1)}, u32[]{:S(2)}) copy-start(f32[128]{0:T(128)S(1)} %broadcast_multiply_fusion.3) | copy-start | bytes 1540
  115.7 14.9 %copy-start.12 = (f32[128]{0:T(128)S(1)}, f32[128]{0:T(128)}, u32[]{:S(2)}) copy-start(f32[128]{0:T(128)} %copy-done.11) | copy-start | bytes 1540
  115.7 14.9 %copy-start.19 = (f32[128]{0:T(128)S(1)}, f32[128]{0:T(128)}, u32[]{:S(2)}) copy-start(f32[128]{0:T(128)} %copy-done.18) | copy-start | bytes 1540
  115.7 15.2 %copy-start.4 = (f32[1,128,768]{2,1,0:T(8,128)S(1)}, f32[1,128,768]{2,1,0:T(8,128)}, u32[]{:S(2)}) copy-start(f32[1,128,768]{2,1,0:T(8,128)} %param.17) | copy-start | bytes 1179652
  148.0 3.3 %copy-start.1 = (bf16[4,128,768]{2,1,0:T(8,128)(2,1)S(1)}, bf16[4,128,768]{2,1,0:T(8,128)(2,1)}, u32[]{:S(2)}) copy-start(bf16[4,128,768]{2,1,0:T(8,128)(2,1)} %shard_map.166) | copy-start | bytes 2359300
  148.1 4.7 %copy-start.20 = (f32[768]{0:T(1024)S(1)}, f32[768]{0:T(1024)}, u32[]{:S(2)}) copy-start(f32[768]{0:T(1024)} %get-tuple-element.97) | copy-start | bytes 9220
  148.1 82.6 %all-gather.6.cloned.1.call-start = ((), (), s32[]{:S(2)}) async-start(), calls=%async_computation.4 | async-start | bytes 1474560 | tf_op jit(solution)/shard_map/all_gather | solution.py:584
  152.8 10.6 %copy-start.6 = (bf16[512,768]{1,0:T(8,128)(2,1)S(1)}, bf16[512,768]{1,0:T(8,128)(2,1)}, u32[]{:S(2)}) copy-start(bf16[512,768]{1,0:T(8,128)(2,1)} %fusion.11) | copy-start | bytes 2359300
  169.5 35.0 %copy-start.16 = (f32[128]{0:T(128)S(1)}, f32[128]{0:T(128)}, u32[]{:S(2)}) copy-start(f32[128]{0:T(128)} %copy-done.15) | copy-start | bytes 1540
  169.5 35.0 %copy-start.21 = (f32[128]{0:T(128)S(1)}, f32[128]{0:T(128)}, u32[]{:S(2)}) copy-start(f32[128]{0:T(128)} %add_rsqrt_fusion.1) | copy-start | bytes 1540
  169.5 35.8 %copy-start.9 = (f32[1,8,96]{2,0,1:T(1,128)S(1)}, f32[1,8,96]{2,0,1:T(1,128)}, u32[]{:S(2)}) copy-start(f32[1,8,96]{2,0,1:T(1,128)} %stack.32) | copy-start | bytes 9220
  202.8 3.4 %copy-start.5 = (bf16[8,96,576]{2,1,0:T(8,128)(2,1)S(1)}, bf16[8,96,576]{2,1,0:T(8,128)(2,1)}, u32[]{:S(2)}) copy-start(bf16[8,96,576]{2,1,0:T(8,128)(2,1)} %get-tuple-element.56) | copy-start | bytes 2654212
  202.8 26.0 %copy-start.7 = (bf16[4,128,768]{2,1,0:T(8,128)(2,1)S(1)}, bf16[4,128,768]{2,1,0:T(8,128)(2,1)}, u32[]{:S(2)}) copy-start(bf16[4,128,768]{2,1,0:T(8,128)(2,1)} %get-tuple-element.54) | copy-start | bytes 2359300
  206.9 21.9 %copy-start.24 = (f32[128]{0:T(128)S(1)}, f32[128]{0:T(128)}, u32[]{:S(2)}) copy-start(f32[128]{0:T(128)} %get-tuple-element.74) | copy-start | bytes 1540
  206.9 22.0 %copy-start.23 = (f32[128]{0:T(128)S(1)}, f32[128]{0:T(128)}, u32[]{:S(2)}) copy-start(f32[128]{0:T(128)} %get-tuple-element.75) | copy-start | bytes 1540
  206.9 22.8 %copy-start.17 = (f32[128]{0:T(128)S(1)}, f32[128]{0:T(128)}, u32[]{:S(2)}) copy-start(f32[128]{0:T(128)} %copy-done.15) | copy-start | bytes 1540
  206.9 22.8 %copy-start.22 = (f32[128]{0:T(128)S(1)}, f32[128]{0:T(128)}, u32[]{:S(2)}) copy-start(f32[128]{0:T(128)} %add_rsqrt_fusion.1) | copy-start | bytes 1540
  (4 other events, 4.9 us)
Sparse Core Ops, SparseCore 0:
  39.5 42.1 all-gather.3
  108.0 41.8 reduce-scatter.6
  152.8 31.0 reduce-scatter.4
  186.2 27.3 all-gather.5

commit v4 on v2

--- a/solution.py
+++ b/solution.py
@@ -299,6 +299,7 @@
 
     copies = []
     relays = []
+    queues = [[] for _ in plan]
     for item, (axis, kind) in enumerate(plan):
         size = sizes[axis]
         if kind == "relay":
@@ -309,11 +310,11 @@
             for step in range(1, half):
                 peer = lax.rem(place + step, half) * 2 + core
                 first = copy(item, step, ins[item], outs[item].at[me[axis]], axis, peer)
-                first.start()
+                queues[item].append(first)
                 origin = lax.rem(place + half - step, half) * 2 + core
                 relays.append((item, step, first, axis, sibling, origin))
             own = copy(item, 0, ins[item], outs[item].at[me[axis]], axis, sibling)
-            own.start()
+            queues[item].append(own)
             copies.append(own)
         elif kind == "spread":
             for rep_step in range(sizes["rep"]):
@@ -323,15 +324,20 @@
                         target = outs[item].at[me["rep"], me["shard"]]
                         slot = rep_step * sizes["shard"] + shard_step
                         one = copy(item, slot, ins[item].at[peer["shard"]], target, None, peer)
-                        one.start()
+                        queues[item].append(one)
                         copies.append(one)
         else:
             for step in range(1, size):
                 peer = lax.rem(me[axis] + step, size)
                 source = ins[item] if kind == "gather" else ins[item].at[peer]
                 one = copy(item, step, source, outs[item].at[me[axis]], axis, peer)
-                one.start()
+                queues[item].append(one)
                 copies.append(one)
+    order = []
+    for item, queue in enumerate(queues):
+        order += [((2 * turn + 1) / len(queue), item, one) for turn, one in enumerate(queue)]
+    for _, _, one in sorted(order, key=lambda entry: entry[:2]):
+        one.start()
     for item, (axis, kind) in enumerate(plan):
         if kind == "swap":
             outs[item][me[axis]] = ins[item][me[axis]]

time: 234 us -> 234 us (level)
  transfers between devices with their start and end apart: 2 -> 2, of which waited for: 0 -> 0; matrix products, arithmetic and copies ran while one was open for 14% -> 14% of each run, Pallas kernels for 28% -> 29%
where the time goes in v4:
time: 234 us; the launch traced here: 233 us
  Pallas kernels  161 us (69%)
  matrix products  23.3 us (10%)
  local copies, waits for them, and re-layouts  18 us (8%)
  other arithmetic  16.4 us (7%)
  between operations  14.5 us (6%)
    pallas_call x7, Pallas kernels, exchange(): pl.pallas_call(functools.partial(exchange_body, plan, sizes), out_shape=s...  145 us
    pallas_call x4, Pallas kernels, local(): pl.pallas_call(kernel, out_shape=shapes, in_specs=[vmem] * len(arrays), o...  15.5 us
    dot_general x4, matrix products, contract_cols(): lax.dot_general(left, right, (((1,), (1,)), ((), ())), preferred_element_...  8.69 us
    dot_general x1, matrix products, split_body(): pre = jnp.dot(c_low, w_up, preferred_element_type=F32) + up_bias  5.67 us
  transfers between devices with their start and end apart: 2, of which 0 were waited for; matrix products, arithmetic and copies ran while one was open for 14% of the time, Pallas kernels for 29%

profile of v4, /device:TPU:0, one launch (start us, length us, event | category | flops | bytes accessed | tf_op | source)
XLA Modules:
  0.0 232.8 jit_solution(4566604417834467122)
XLA Ops:
  8.7 1.7 fusion.48
  10.4 1.4 concatenate.16.refs_2_
  11.8 2.3 shard_map.160
  14.1 30.8 %shard_map.161 = (bf16[8,96,576]{2,1,0:T(8,128)(2,1)}, bf16[8,96,768]{2,1,0:T(8,128)(2,1)}, bf16[8,1,1152]{2,1,0:T(2,128)(2,1)}, bf16[4,128,768]{2,1,0:T(8,128)(2,1)}, bf16[4,128,768]{2,1,0:T(8,128)(2,1)}) custom-call(bf16[96,576]{1,0:T(8,128)(2,1)} %get-tuple-element.33.refs_0_, bf16[96,768]{1,0:T(8,128)(2,1)} %bitcast.107, ...), custom_call_target="tpu_custom_call" | custom-call | tf_op jit(solution)/shard_map/pallas_call | solution.py:373
  46.9 1.4 convert_reduce_fusion.5
  49.1 1.6 fusion.19.qkv
  50.7 4.2 %shard_map.162 = (bf16[512,192]{1,0:T(8,128)(2,1)}, f32[512,3]{1,0:T(8,128)}) custom-call(bf16[512,576]{1,0:T(8,128)(2,1)} %fusion.19.qkv), custom_call_target="tpu_custom_call" | custom-call | tf_op jit(solution)/shard_map/pallas_call | solution.py:388
  54.9 16.0 %shard_map.163 = bf16[4,512,192]{2,1,0:T(8,128)(2,1)} custom-call(bf16[512,192]{1,0:T(8,128)(2,1)} %get-tuple-element.39.refs_0_), custom_call_target="tpu_custom_call" | custom-call | tf_op jit(solution)/shard_map/pallas_call | solution.py:373
  70.8 1.0 dynamic-slice_bitcast_fusion
  73.5 13.7 %shard_map.164 = bf16[4,128,768]{2,1,0:T(8,128)(2,1)} custom-call(bf16[128,768]{1,0:T(8,128)(2,1)} %add_convert_fusion.1.refs_0_), custom_call_target="tpu_custom_call" | custom-call | tf_op jit(solution)/shard_map/pallas_call | solution.py:373
  87.3 5.7 %fusion.7 = (bf16[512,768]{1,0:T(8,128)(2,1)S(1)}, f32[512,768]{1,0:T(8,128)S(1)}) fusion(f32[768]{0:T(1024)S(1)} %add.146, bf16[512,768]{1,0:T(8,128)(2,1)} %bitcast.98, bf16[768,1536]{1,0:T(8,128)(2,1)} %all-gather.2.cloned.1.call-done), kind=kOutput, calls=%fused_computation.14 | convolution fusion | flops 629932032 | bytes 4328448 | tf_op jit(solution)/shard_map/dot_general | solution.py:547
  93.0 1.1 fusion.50
  96.0 1.6 pad_maximum_fusion
  97.8 1.0 copy-done.3
  98.9 1.2 copy.36
  100.5 1.3 fusion.11
  102.1 3.0 %convolution_convert_fusion.4 = bf16[512,768]{1,0:T(8,128)(2,1)} fusion(bf16[768,1536]{1,0:T(8,128)(2,1)} %all-gather.2.cloned.1.call-done, bf16[512,768]{1,0:T(8,128)(2,1)S(1)} %copy-done.16), kind=kOutput, calls=%fused_computation.45 | convolution fusion | flops 604372992 | bytes 2752512 | tf_op jit(solution)/shard_map/dot_general | solution.py:50
  105.1 14.2 %shard_map.165 = bf16[4,128,768]{2,1,0:T(8,128)(2,1)} custom-call(bf16[4,128,768]{2,1,0:T(8,128)(2,1)} %bitcast.96), custom_call_target="tpu_custom_call" | custom-call | tf_op jit(solution)/shard_map/pallas_call | solution.py:373
  119.4 1.5 convert_reduce_fusion.2
  122.2 13.9 %shard_map.166 = bf16[4,128,768]{2,1,0:T(8,128)(2,1)} custom-call(bf16[128,768]{1,0:T(8,128)(2,1)} %convert_element_type.93.refs_0_), custom_call_target="tpu_custom_call" | custom-call | tf_op jit(solution)/shard_map/pallas_call | solution.py:373
  136.1 1.6 copy.37
  137.8 1.4 convolution_convert_fusion.7
  140.0 5.5 %shard_map.167 = (bf16[512,576]{1,0:T(8,128)(2,1)}, f32[1,192]{1,0:T(1,128)}, f32[1,192]{1,0:T(1,128)}) custom-call(bf16[512,576]{1,0:T(8,128)(2,1)} %fusion.19.qkv, bf16[512,192]{1,0:T(8,128)(2,1)} %copy.33.upstream, f32[512,3]{1,0:T(8,128)} %get-tuple-element.43.lse), custom_call_target="tpu_custom_call" | custom-call | tf_op jit(solution)/shard_map/pallas_call | solution.py:388
  147.8 2.0 convolution_convert_fusion.2
  149.9 1.5 copy.38
  151.4 3.2 %convolution_convert_fusion.5 = bf16[512,768]{1,0:T(8,128)(2,1)} fusion(bf16[512,576]{1,0:T(8,128)(2,1)} %get-tuple-element.44, bf16[768,576]{1,0:T(8,128)(2,1)} %bitcast.115), kind=kOutput, calls=%fused_computation.46 | convolution fusion | flops 453378048 | bytes 2260992 | tf_op jit(solution)/shard_map/dot_general | solution.py:50
  154.6 2.8 %convolution_convert_fusion.3 = bf16[512,768]{1,0:T(8,128)(2,1)} fusion(bf16[512,768]{1,0:T(8,128)(2,1)} %copy-done.14, bf16[768,1536]{1,0:T(8,128)(2,1)S(1)} %copy-done.11), kind=kOutput, calls=%fused_computation.44 | convolution fusion | flops 604372992 | bytes 2752512 | tf_op jit(solution)/shard_map/dot_general | solution.py:549
  157.4 41.7 %shard_map.168 = (bf16[4,128,768]{2,1,0:T(8,128)(2,1)}, bf16[4,128,768]{2,1,0:T(8,128)(2,1)}, bf16[4,96,1536]{2,1,0:T(8,128)(2,1)}, bf16[8,96,768]{2,1,0:T(8,128)(2,1)}) custom-call(bf16[4,128,768]{2,1,0:T(8,128)(2,1)} %bitcast.97, bf16[4,128,768]{2,1,0:T(8,128)(2,1)} %bitcast.100, bf16[96,1536]{1,0:T(8,128)(2,1)} %reduce-scatter.2.cloned.1.call-done.refs_2_, ...), custom_call_target="tpu_custom_call" | custom-call | tf_op jit(solution)/shard_map/pallas_call | solution.py:373
  199.2 1.6 convert_reduce_fusion
  202.8 14.7 %shard_map.169 = (bf16[4,96,768]{2,1,0:T(8,128)(2,1)}, f32[4,8,1,1152]{3,2,1,0:T(1,128)}) custom-call(bf16[96,768]{1,0:T(8,128)(2,1)} %reduce_sum.216.refs_0_, f32[8,1,1152]{2,1,0:T(1,128)} %broadcast_in_dim.43.refs_1_), custom_call_target="tpu_custom_call" | custom-call | tf_op jit(solution)/shard_map/pallas_call | solution.py:373
  217.5 1.0 reduce_sum.224
  222.4 3.5 %shard_map.170 = (f32[96,2304]{1,0:T(8,128)}, f32[96,768]{1,0:T(8,128)}, f32[96,3072]{1,0:T(8,128)}, f32[384,768]{1,0:T(8,128)}) custom-call(bf16[4,96,768]{2,1,0:T(8,128)(2,1)} %get-tuple-element.50.attn_all, bf16[4,96,1536]{2,1,0:T(8,128)(2,1)} %get-tuple-element.51.ff_all), custom_call_target="tpu_custom_call" | custom-call | tf_op jit(solution)/shard_map/pallas_call | solution.py:388
  (121 shorter events, 19.2 us)
Async XLA Ops:
  7.2 80.1 %all-gather.2.cloned.1.call-start = ((), (), s32[]{:S(2)}) async-start(), calls=%async_computation.1 | async-start | bytes 2654208 | tf_op jit(solution)/shard_map/all_gather | solution.py:516
  44.8 3.5 %copy-start = (bf16[4,128,768]{2,1,0:T(8,128)(2,1)S(1)}, bf16[4,128,768]{2,1,0:T(8,128)(2,1)}, u32[]{:S(2)}) copy-start(bf16[4,128,768]{2,1,0:T(8,128)(2,1)} %get-tuple-element.34) | copy-start | bytes 2359300
  44.9 112.5 %reduce-scatter.2.cloned.1.call-start = ((), (), s32[]{:S(2)}) async-start(), calls=%async_computation.2 | async-start | bytes 2654208 | tf_op jit(solution)/shard_map/reduce_scatter | solution.py:557
  46.9 2.2 copy-start.12
  50.7 21.3 %copy-start.2 = (bf16[1,128,768]{2,1,0:T(8,128)(2,1)S(1)}, bf16[1,128,768]{2,1,0:T(8,128)(2,1)}, u32[]{:S(2)}) copy-start(bf16[1,128,768]{2,1,0:T(8,128)(2,1)} %param.9) | copy-start | bytes 589828
  50.7 21.3 %copy-start.5 = (bf16[8,96,768]{2,1,0:T(8,128)(2,1)S(1)}, bf16[8,96,768]{2,1,0:T(8,128)(2,1)}, u32[]{:S(2)}) copy-start(bf16[8,96,768]{2,1,0:T(8,128)(2,1)} %get-tuple-element.40) | copy-start | bytes 3538948
  87.2 5.7 %copy-start.10 = (bf16[768,1536]{1,0:T(8,128)(2,1)S(1)}, bf16[768,1536]{1,0:T(8,128)(2,1)}, u32[]{:S(2)}) copy-start(bf16[768,1536]{1,0:T(8,128)(2,1)} %all-gather.2.cloned.1.call-done) | copy-start | bytes 7077892
  87.3 5.7 %copy-start.13 = (bf16[4,128,768]{2,1,0:T(8,128)(2,1)S(1)}, bf16[4,128,768]{2,1,0:T(8,128)(2,1)}, u32[]{:S(2)}) copy-start(bf16[4,128,768]{2,1,0:T(8,128)(2,1)} %get-tuple-element.41) | copy-start | bytes 2359300
  92.9 2.3 copy-start.14
  93.0 1.4 copy-start.9
  94.1 1.1 copy-start.15
  97.7 1.2 copy-start.3
  100.1 2.0 copy-start.16
  105.1 16.2 %copy-start.6 = (f32[1,128,768]{2,1,0:T(8,128)S(1)}, f32[1,128,768]{2,1,0:T(8,128)}, u32[]{:S(2)}) copy-start(f32[1,128,768]{2,1,0:T(8,128)} %param.17) | copy-start | bytes 1179652
  136.1 1.6 copy-start.1
  139.1 8.3 %copy-start.4 = (bf16[4,192,512]{2,1,0:T(8,128)(2,1)S(1)}, bf16[4,192,512]{2,1,0:T(8,128)(2,1)}, u32[]{:S(2)}) copy-start(bf16[4,192,512]{2,1,0:T(8,128)(2,1)} %copy.36) | copy-start | bytes 2359300
  151.4 3.3 %copy-start.11 = (bf16[768,1536]{1,0:T(8,128)(2,1)S(1)}, bf16[768,1536]{1,0:T(8,128)(2,1)}, u32[]{:S(2)}) copy-start(bf16[768,1536]{1,0:T(8,128)(2,1)} %all-gather.2.cloned.1.call-done) | copy-start | bytes 7077892
  199.2 2.8 %copy-start.7 = (bf16[8,96,768]{2,1,0:T(8,128)(2,1)S(1)}, bf16[8,96,768]{2,1,0:T(8,128)(2,1)}, u32[]{:S(2)}) copy-start(bf16[8,96,768]{2,1,0:T(8,128)(2,1)} %get-tuple-element.47) | copy-start | bytes 3538948
  200.7 18.5 %copy-start.8 = (bf16[4,128,768]{2,1,0:T(8,128)(2,1)S(1)}, bf16[4,128,768]{2,1,0:T(8,128)(2,1)}, u32[]{:S(2)}) copy-start(bf16[4,128,768]{2,1,0:T(8,128)(2,1)} %get-tuple-element.45) | copy-start | bytes 2359300
Sparse Core Ops, SparseCore 0:
  45.0 36.1 all-gather.1
  97.8 42.7 reduce-scatter.1
